TPU v7x, 32 devices: a whole 2x2x4 slice. The times are simulated.
32 devices in a mesh: side: 4 (over y, x), edge: 8 (over z, core).
Axes of the slice: x: 2, y: 2, z: 4, core: 2. Of those that a mesh axis runs over, the one named last changes fastest.
Arguments:
- parent_blocks: bfloat16 [32, 450, 128], P(('side', 'edge')), may hold values from -6 to 6
- interp_weight: bfloat16 [128, 2, 128, 128], P(('side', 'edge')), may hold values from -0.375 to 0.375
- tile_source: int32 [128, 2], P(('side', 'edge')), may hold values from 0 to 31, as said below
- destination: int32 [16384, 1], P(('side', 'edge')), may hold values from 0 to 7; in each aligned block of 512 rows (0 to 511, 512 to 1023, ...) at most 128 rows name the same one
- remap_matrix: bfloat16 [5, 400, 90], replicated, may hold values from -0.625 to 0.625
Outputs:
- forcing: bfloat16 [5, 400, 32768], P(None, None, ('side', 'edge'))
Inputs may be any that keep to these rules, and one draw needn't show every extreme that they name: `tile_source`: the two blocks of a tile are distinct, and each is the tile's own device d or d - 1 or d + 1 modulo 32 along the loop of devices. `destination`: among the rows of one device no owner is named more than 128 times, and in some devices some owner is named exactly 128 times.
All inputs are finite; a program needn't handle non-finite values.
Results may differ from a plain program's by a relative error of at most 0.0049.
Values may be sent and summed in bfloat16 or wider, within the bound.
No kernel may reach another device: no remote copies, remote signals or barrier semaphores. Data moves between devices by JAX's collectives and lax.ppermute only.
A program may use at most 64 MiB of HBM per device.

v0:
```python
import jax
import jax.numpy as jnp
from jax import lax
from jax.sharding import PartitionSpec as P


def padded(array, sides, width):
    for axis, dim in sides:
        devices, length = (lax.axis_size(axis), array.shape[dim])
        up = [(i, (i + 1) % devices) for i in range(devices)]
        down = [(j, i) for i, j in up]
        last = lax.slice_in_dim(array, length - width, length, axis=dim)
        leading = lax.slice_in_dim(array, 0, width, axis=dim)
        before = lax.ppermute(last, axis, up)
        after = lax.ppermute(leading, axis, down)
        array = jnp.concatenate([before, array, after], axis=dim)
    return array


def remap_rows(remap_matrix, rows):
    shaped = rows.reshape(remap_matrix.shape[0], remap_matrix.shape[2], rows.shape[1])
    result = jnp.einsum("vcl,vln->vcn", remap_matrix, shaped, preferred_element_type=jnp.float32)
    return result.astype(jnp.bfloat16)


def body(parent_blocks, interp_weight, tile_source, destination, remap_matrix):
    edge_count = lax.axis_size("edge")
    block_count = lax.axis_size("side") * edge_count
    position = lax.axis_index("side") * edge_count + lax.axis_index("edge")
    rim_blocks = padded(parent_blocks, ((("side", "edge"), 0),), 1)
    offset = (tile_source - position + 1 + block_count) % block_count
    chosen = rim_blocks[offset]
    summed = jnp.einsum("tkfp,tkpr->tfr", chosen, interp_weight, preferred_element_type=jnp.float32)
    coarse = summed.astype(jnp.bfloat16)
    tile_count, feat_count, tile_rows = coarse.shape
    rows = coarse.transpose(1, 0, 2).reshape(feat_count, tile_count * tile_rows)
    row_count = destination.shape[0]
    capacity = max(2, 2 * row_count // edge_count)
    owners = destination[:, 0]
    owner_hits = (owners[:, None] == jnp.arange(edge_count, dtype=jnp.int32)[None, :]).astype(
        jnp.int32
    )
    places = jnp.sum(jnp.cumsum(owner_hits, axis=0) * owner_hits, axis=1) - 1
    slot_index = owners * capacity + places
    outbox = (
        jnp.zeros((feat_count, edge_count * capacity), jnp.bfloat16).at[:, slot_index].set(rows)
    )
    inbox = lax.all_to_all(outbox, "edge", split_axis=1, concat_axis=1, tiled=True)
    forcing = remap_rows(remap_matrix, inbox)
    return forcing


def solution(mesh):
    return jax.shard_map(
        body,
        mesh=mesh,
        in_specs=(
            P(("side", "edge"), None, None),
            P(("side", "edge"), None, None, None),
            P(("side", "edge"), None),
            P(("side", "edge"), None),
            P(),
        ),
        out_specs=P(None, None, ("side", "edge")),
        check_vma=False,
    )
```

profile of v0, /device:TPU:0, one launch (start us, length us, event | category | flops | bytes accessed | tf_op | source)
XLA Modules:
  0.0 49.2 jit_solution(1207886696506333563)
XLA Ops:
  0.0 0.0 copy-start
  0.0 0.5 collective-permute-start
  0.5 6.0 %collective-permute-start.1 = (bf16[1,450,128]{2,1,0:T(8,128)(2,1)}, bf16[1,450,128]{2,1,0:T(8,128)(2,1)S(1)}, u32[]{:S(2)}, u32[]{:S(2)}) collective-permute-start(bf16[1,450,128]{2,1,0:T(8,128)(2,1)} %param.5), channel_id=1, source_target_pairs={{1,0},{2,1},{3,2},{4,3},{5,4},{6,5},{7,6},{8,7},{9,8},{10,9},{11,1... | collective-permute-start | bytes 345608 | tf_op jit(solution)/shard_map/ppermute | solution.py:15
  6.4 0.7 %fusion.5 = s32[8,4,128]{2,0,1:T(8,128)S(1)} fusion(s32[4,128]{1,0:T(4,128)} %bitcast.37), kind=kLoop, calls=%fused_computation.14 | loop fusion | flops 8192 | bytes 18432 | tf_op jit(solution)/shard_map/convert_element_type | solution.py:40
  7.1 1.1 %reduce-window.6 = s32[8,4,128]{2,0,1:T(8,128)S(1)} reduce-window(s32[8,4,128]{2,0,1:T(8,128)S(1)} %fusion.5, s32[]{:T(128)} %constant.21.clone.1), window={size=1x1x128 pad=0_0x0_0x127_0}, to_apply=%region_0.1 | reduce-window | flops 520192 | bytes 32772 | tf_op jit(solution)/shard_map/reduce-window
  8.2 0.2 slice_reduce_fusion
  8.5 0.8 %fusion.4 = s32[512]{0:T(512)S(1)} fusion(s32[8,4,128]{2,0,1:T(8,128)S(1)} %reduce-window.6, s32[8,4]{0,1:T(4,128)S(1)} %slice.7, s32[512]{0:T(512)} %bitcast.38), kind=kLoop, calls=%fused_computation.11 | loop fusion | flops 15872 | bytes 20608 | tf_op jit(solution)/shard_map/reduce_sum | solution.py:43
  9.3 0.7 %compare_select_fusion = s32[512,1]{0,1:T(1,128)S(1)} fusion(s32[512,1]{0,1:T(1,128)S(1)} %bitcast.39, s32[512,1]{0,1:T(1,128)} %param.8), kind=kLoop, calls=%fused_computation.15 | loop fusion | flops 2560 | bytes 6144 | tf_op jit(solution)/shard_map/select_n | solution.py:46
  10.0 0.7 %compare_select_fusion.1 = s32[4,2]{0,1:T(2,128)S(1)} fusion(s32[4,2]{0,1:T(2,128)} %param.7, s32[]{:T(128)S(6)} %add.43), kind=kLoop, calls=%fused_computation.17 | loop fusion | flops 128 | bytes 68 | tf_op jit(solution)/shard_map/select_n | solution.py:32
  10.7 0.1 copy.12
  10.8 0.1 reshape.39
  10.9 0.0 collective-permute-done
  10.9 0.0 collective-permute-done.1
  10.9 0.9 %pad_maximum_fusion = bf16[3,450,128]{2,1,0:T(8,128)(2,1)S(1)} fusion(bf16[1,450,128]{2,1,0:T(8,128)(2,1)S(1)} %collective-permute-done.1, bf16[1,450,128]{2,1,0:T(8,128)(2,1)} %param.5, bf16[1,450,128]{2,1,0:T(8,128)(2,1)S(1)} %collective-permute-done), kind=kLoop, calls=%fused_computation.8 | loop fusion | flops 345600 | bytes 691200 | tf_op jit(solution)/shard_map/concatenate | solution.py:16
  11.8 0.7 %gather_fusion = bf16[8,450,128]{2,1,0:T(8,128)(2,1)S(1)} fusion(bf16[3,450,128]{2,1,0:T(8,128)(2,1)S(1)} %pad_maximum_fusion, s32[1024]{0:T(1024)S(1)} %pad_clamp_fusion), kind=kCustom, calls=%fused_computation | custom fusion | bytes 1843232 | tf_op jit(solution)/shard_map/gather | solution.py:32
  12.5 1.4 %fusion.1 = bf16[450,4,128]{2,0,1:T(8,128)(2,1)S(1)} fusion(bf16[4,2,450,128]{3,2,1,0:T(8,128)(2,1)S(1)} %bitcast.34, bf16[4,2,128,128]{3,2,1,0:T(8,128)(2,1)} %param.6), kind=kOutput, calls=%fused_computation.5 | convolution fusion | flops 118195200 | bytes 1644544 | tf_op jit(solution)/shard_map/tkfp,tkpr->tfr/dot_general | solution.py:33
  13.9 0.2 copy.13
  14.1 0.2 pad.4
  14.3 0.1 copy.18
  14.4 0.2 copy.14
  14.6 2.7 %scatter_custom_fusion = bf16[450,1024]{0,1:T(8,128)(2,1)S(1)} fusion(s32[512]{0:T(512)S(1)} %bitcast.40, bf16[512,450]{1,0:T(8,128)(2,1)S(1)} %copy.14, bf16[]{:T(256)} %constant.16.clone.1), kind=kCustom, calls=%fused_computation.6 | custom fusion | bytes 921602 | tf_op jit(solution)/shard_map/scatter | solution.py:46
  17.3 0.6 %copy.15 = bf16[450,8,128]{2,0,1:T(8,128)(2,1)S(1)} copy(bf16[450,8,128]{0,2,1:T(8,128)(2,1)S(1)} %bitcast.33) | data formatting | bytes 1843200 | tf_op jit(solution)/shard_map/all_to_all | solution.py:48
  18.0 27.4 %all_to_all.9 = bf16[450,8,128]{2,0,1:T(8,128)(2,1)S(1)} all-to-all(bf16[450,8,128]{2,0,1:T(8,128)(2,1)S(1)} %copy.15), channel_id=1, replica_groups=mesh['side'=4,'edge'=8] {'edge'}, dimensions={1} | all-to-all | bytes 1843200 | tf_op jit(solution)/shard_map/all_to_all | solution.py:48
  45.4 0.1 copy.16
  45.5 0.4 reshape.36
  45.9 0.0 copy-done
  45.9 3.2 %convert_bitcast_fusion = bf16[5,400,1024]{2,1,0:T(8,128)(2,1)} fusion(bf16[5,90,1024]{2,1,0:T(8,128)(2,1)S(1)} %reshape.36, bf16[5,400,90]{1,2,0:T(8,128)(2,1)S(1)} %copy-done), kind=kOutput, calls=%fused_computation.2 | convolution fusion | flops 370688000 | bytes 5377600 | tf_op jit(solution)/shard_map/vcl,vln->vcn/dot_general | solution.py:22
  (4 shorter events, 0.1 us)
Async XLA Ops:
  0.0 45.9 %copy-start = (bf16[5,400,90]{1,2,0:T(8,128)(2,1)S(1)}, bf16[5,400,90]{1,2,0:T(8,128)(2,1)}, u32[]{:S(2)}) copy-start(bf16[5,400,90]{1,2,0:T(8,128)(2,1)} %param.9) | copy-start | bytes 1080004
  0.0 10.9 %collective-permute-start = (bf16[1,450,128]{2,1,0:T(8,128)(2,1)}, bf16[1,450,128]{2,1,0:T(8,128)(2,1)S(1)}, u32[]{:S(2)}, u32[]{:S(2)}) collective-permute-start(bf16[1,450,128]{2,1,0:T(8,128)(2,1)} %param.5), channel_id=1, source_target_pairs={{0,1},{1,2},{2,3},{3,4},{4,5},{5,6},{6,7},{7,8},{8,9},{9,10},{10,1... | collective-permute-start | bytes 345608 | tf_op jit(solution)/shard_map/ppermute | solution.py:14
  0.5 10.4 %collective-permute-start.1 = (bf16[1,450,128]{2,1,0:T(8,128)(2,1)}, bf16[1,450,128]{2,1,0:T(8,128)(2,1)S(1)}, u32[]{:S(2)}, u32[]{:S(2)}) collective-permute-start(bf16[1,450,128]{2,1,0:T(8,128)(2,1)} %param.5), channel_id=1, source_target_pairs={{1,0},{2,1},{3,2},{4,3},{5,4},{6,5},{7,6},{8,7},{9,8},{10,9},{11,1... | collective-permute-start | bytes 345608 | tf_op jit(solution)/shard_map/ppermute | solution.py:15
where the time goes:
time: 49.4 us; the launch traced here: 49.2 us
  blocking collectives  27.4 us (55%)
  starting transfers between devices  6.43 us (13%)
  local copies, waits for them, and re-layouts  5.66 us (11%)
  other arithmetic  4.95 us (10%)
  matrix products  4.61 us (9%)
    all_to_all x1, blocking collectives, body(): lax.all_to_all(outbox, 'edge', split_axis=1, concat_axis=1, tiled=True)  27.4 us
    ppermute x1, starting transfers between devices, padded(): after = lax.ppermute(leading, axis, down)  5.98 us
    dot_general x1, matrix products, remap_rows(): jnp.einsum('vcl,vln->vcn', remap_matrix, shaped, preferred_element_type=j...  3.24 us
    scatter x1, local copies, waits for them, and re-layouts, body(): jnp.zeros((feat_count, edge_count * capacity), jnp.bfloat16)  2.74 us
    dot_general x1, matrix products, body(): jnp.einsum('tkfp,tkpr->tfr', chosen, interp_weight, preferred_element_typ...  1.36 us
    another operation x2, other arithmetic  1.16 us
  transfers between devices with their start and end apart: 2, of which 0 were waited for; matrix products, arithmetic and copies ran while one was open for 9% of the time, Pallas kernels for 0%

commit v1 on v0

v1 whole, which is shorter than its diff:
```python
import functools

import jax
import jax.numpy as jnp
from jax import lax
from jax.experimental import pallas as pl
from jax.experimental.pallas import tpu as pltpu
from jax.sharding import PartitionSpec as P

AXES = ("side", "edge")
VMEM = pl.BlockSpec(memory_space=pltpu.VMEM)
SMEM = pl.BlockSpec(memory_space=pltpu.SMEM)


def neighbours(block):
    count = lax.axis_size(AXES)
    up = [(i, (i + 1) % count) for i in range(count)]
    down = [(j, i) for i, j in up]
    return lax.ppermute(block, AXES, up), lax.ppermute(block, AXES, down)


def slot_rows(owner_count, capacity, dest):
    tiles, lanes = dest.shape
    owner = lax.broadcasted_iota(jnp.int32, (owner_count, lanes), 0)
    hits = [(dest[t : t + 1, :] == owner).astype(jnp.float32) for t in range(tiles)]
    earlier = (
        lax.broadcasted_iota(jnp.int32, (lanes, lanes), 0)
        < lax.broadcasted_iota(jnp.int32, (lanes, lanes), 1)
    ).astype(jnp.bfloat16)
    stacked = jnp.concatenate(hits, axis=0).astype(jnp.bfloat16)
    before = jnp.dot(stacked, earlier, preferred_element_type=jnp.float32)
    carry = jnp.zeros((owner_count, 1), jnp.float32)
    slots = []
    for t in range(tiles):
        place = before[t * owner_count : (t + 1) * owner_count, :] + carry
        rank = jnp.sum(hits[t] * place, axis=0, keepdims=True)
        slots.append(dest[t : t + 1, :] * capacity + rank.astype(jnp.int32))
        carry = carry + jnp.sum(hits[t], axis=1, keepdims=True)
    return slots


def select_kernel(sizes, source_ref, dest_ref, weight_ref, out_ref, spread_ref):
    owner_count, capacity, block_count = sizes
    tiles, _, pcol, rows = weight_ref.shape
    position = lax.axis_index("side") * owner_count + lax.axis_index("edge")
    slots = slot_rows(owner_count, capacity, dest_ref[...])
    spread_ref[...] = jnp.zeros_like(spread_ref)
    for t in range(tiles):
        for k in range(2):
            offset = lax.rem(source_ref[k, t] - position + 1 + block_count, block_count)
            place = pl.multiple_of(offset * pcol, pcol)
            spread_ref[pl.ds(place, pcol), t * rows : (t + 1) * rows] = weight_ref[t, k]
    step = 256
    for c in range(owner_count * capacity // step):
        slot = lax.broadcasted_iota(jnp.int32, (step, rows), 0) + c * step
        chosen = jnp.concatenate(
            [(slot == slots[t]).astype(jnp.float32).astype(jnp.bfloat16) for t in range(tiles)],
            axis=1,
        )
        picked = lax.dot_general(
            spread_ref[...], chosen, (((1,), (1,)), ((), ())), preferred_element_type=jnp.float32
        )
        out_ref[:, c * step : (c + 1) * step] = picked.astype(jnp.bfloat16)


def interpolate_kernel(capacity, before_ref, own_ref, after_ref, weight_ref, out_ref):
    parents = jnp.concatenate([before_ref[0], own_ref[0], after_ref[0]], axis=1)
    pair = 2
    for c in range(out_ref.shape[0] // pair):
        width = pair * capacity
        coarse = jnp.dot(
            parents,
            weight_ref[:, c * width : (c + 1) * width],
            preferred_element_type=jnp.float32,
        ).astype(jnp.bfloat16)
        for i in range(pair):
            out_ref[c * pair + i] = coarse[:, i * capacity : (i + 1) * capacity]


def remap_kernel(inbox_ref, remap_ref, out_ref):
    variables, levels, _ = remap_ref.shape
    for v in range(variables):
        rows = jnp.concatenate(
            [inbox_ref[i, v * levels : (v + 1) * levels, :] for i in range(inbox_ref.shape[0])],
            axis=1,
        )
        result = lax.dot_general(
            remap_ref[v], rows, (((0,), (0,)), ((), ())), preferred_element_type=jnp.float32
        )
        out_ref[v] = result.astype(jnp.bfloat16)


def kernel_body(parent_blocks, interp_weight, tile_source, destination, remap_matrix):
    edge_count = lax.axis_size("edge")
    block_count = lax.axis_size(AXES)
    tiles, _, pcol, tile_rows = interp_weight.shape
    features = parent_blocks.shape[1]
    variables, child_levels, levels = remap_matrix.shape
    capacity = 2 * destination.shape[0] // edge_count
    slots = edge_count * capacity

    before, after = neighbours(parent_blocks)
    weights = pl.pallas_call(
        functools.partial(select_kernel, (edge_count, capacity, block_count)),
        out_shape=jax.ShapeDtypeStruct((3 * pcol, slots), jnp.bfloat16),
        in_specs=[SMEM, VMEM, VMEM],
        out_specs=VMEM,
        scratch_shapes=[pltpu.VMEM((3 * pcol, tiles * tile_rows), jnp.bfloat16)],
        cost_estimate=pl.CostEstimate(
            flops=2 * 3 * pcol * tiles * tile_rows * slots,
            bytes_accessed=2 * 3 * pcol * slots,
            transcendentals=0,
        ),
        name="select_weights",
    )(tile_source.T, destination.reshape(tiles, tile_rows), interp_weight)
    outbox = pl.pallas_call(
        functools.partial(interpolate_kernel, capacity),
        out_shape=jax.ShapeDtypeStruct((edge_count, features, capacity), jnp.bfloat16),
        in_specs=[VMEM] * 4,
        out_specs=VMEM,
        cost_estimate=pl.CostEstimate(
            flops=2 * 3 * pcol * features * slots,
            bytes_accessed=2 * features * slots,
            transcendentals=0,
        ),
        name="interpolate",
    )(before, parent_blocks, after, weights)
    inbox = lax.all_to_all(outbox, "edge", split_axis=0, concat_axis=0, tiled=True)
    pair = 2
    return pl.pallas_call(
        remap_kernel,
        grid=(edge_count // pair,),
        out_shape=jax.ShapeDtypeStruct((variables, child_levels, slots), jnp.bfloat16),
        in_specs=[
            pl.BlockSpec((pair, features, capacity), lambda i: (i, 0, 0)),
            pl.BlockSpec((variables, levels, child_levels), lambda i: (0, 0, 0)),
        ],
        out_specs=pl.BlockSpec((variables, child_levels, pair * capacity), lambda i: (0, 0, i)),
        cost_estimate=pl.CostEstimate(
            flops=2 * variables * child_levels * levels * slots,
            bytes_accessed=2 * variables * child_levels * slots,
            transcendentals=0,
        ),
        name="remap",
    )(inbox, jnp.swapaxes(remap_matrix, 1, 2))


def plain_body(parent_blocks, interp_weight, tile_source, destination, remap_matrix):
    edge_count = lax.axis_size("edge")
    block_count = lax.axis_size(AXES)
    position = lax.axis_index(AXES)
    before, after = neighbours(parent_blocks)
    rim_blocks = jnp.concatenate([before, parent_blocks, after], axis=0)
    offset = (tile_source - position + 1 + block_count) % block_count
    chosen = rim_blocks[offset]
    summed = jnp.einsum(
        "tkfp,tkpr->tfr", chosen, interp_weight, preferred_element_type=jnp.float32
    )
    coarse = summed.astype(jnp.bfloat16)
    tile_count, feat_count, tile_rows = coarse.shape
    rows = coarse.transpose(1, 0, 2).reshape(feat_count, tile_count * tile_rows)
    row_count = destination.shape[0]
    capacity = max(2, 2 * row_count // edge_count)
    owners = destination[:, 0]
    owner_hits = (owners[:, None] == jnp.arange(edge_count, dtype=jnp.int32)[None, :]).astype(
        jnp.int32
    )
    places = jnp.sum(jnp.cumsum(owner_hits, axis=0) * owner_hits, axis=1) - 1
    slot_index = owners * capacity + places
    outbox = (
        jnp.zeros((feat_count, edge_count * capacity), jnp.bfloat16).at[:, slot_index].set(rows)
    )
    inbox = lax.all_to_all(outbox, "edge", split_axis=1, concat_axis=1, tiled=True)
    shaped = inbox.reshape(remap_matrix.shape[0], remap_matrix.shape[2], inbox.shape[1])
    result = jnp.einsum("vcl,vln->vcn", remap_matrix, shaped, preferred_element_type=jnp.float32)
    return result.astype(jnp.bfloat16)


def solution(mesh):
    body = kernel_body if mesh.shape["edge"] == 8 else plain_body
    return jax.shard_map(
        body,
        mesh=mesh,
        in_specs=(
            P(AXES, None, None),
            P(AXES, None, None, None),
            P(AXES, None),
            P(AXES, None),
            P(),
        ),
        out_specs=P(None, None, AXES),
        check_vma=False,
    )
```

time: 49.4 us -> 47.4 us (0.960)
  Pallas kernels: 0 us -> 10.5 us
  other arithmetic: 4.95 us -> 0 us
  matrix products: 4.61 us -> 0 us
  local copies, waits for them, and re-layouts: 5.66 us -> 1.28 us
  blocking collectives: 27.4 us -> 28.8 us
    pallas_call x0 -> x3, Pallas kernels: none -> 10.5 us  [the longest x1 4.98 us: kernel_body(): pl.pallas_call(remap_kernel, grid=(edge_count // pair,), out_shape=jax.Sh...]
    dot_general x2 -> x0, matrix products: 4.61 us -> none  [the longest x1 3.24 us: remap_rows(): jnp.einsum('vcl,vln->vcn', remap_matrix, shaped, preferred_element_type=j...]
    scatter x1 -> x0, local copies, waits for them, and re-layouts: 2.74 us -> none  [body(): jnp.zeros((feat_count, edge_count * capacity), jnp.bfloat16)]
    all_to_all x1, blocking collectives: 27.4 us -> 28.8 us  [kernel_body(): lax.all_to_all(outbox, 'edge', split_axis=0, concat_axis=0, tiled=True)]
    select_n x2 -> x0, other arithmetic: 1.38 us -> none  [the longest x1 0.69 us: body(): chosen = rim_blocks[offset]]
    another operation x2 -> x0, other arithmetic: 1.16 us -> none
    unnamed x4, local copies, waits for them, and re-layouts: 0.26 us -> 1.28 us
    concatenate x1 -> x0, other arithmetic: 0.93 us -> none  [padded(): array = jnp.concatenate([before, array, after], axis=dim)]
  transfers between devices with their start and end apart: 2 -> 2, of which waited for: 0 -> 1; matrix products, arithmetic and copies ran while one was open for 9% -> 0% of each run, Pallas kernels for 0% -> 6%
where the time goes in v1:
time: 47.4 us; the launch traced here: 47.1 us
  blocking collectives  28.8 us (61%)
  Pallas kernels  10.5 us (22%)
  starting transfers between devices  6.37 us (13%)
  local copies, waits for them, and re-layouts  1.28 us (3%)
    all_to_all x1, blocking collectives, kernel_body(): lax.all_to_all(outbox, 'edge', split_axis=0, concat_axis=0, tiled=True)  28.8 us
    ppermute x2, starting transfers between devices, neighbours(): return (lax.ppermute(block, AXES, up), lax.ppermute(block, AXES, down))  6.37 us
    pallas_call x1, Pallas kernels, kernel_body(): pl.pallas_call(remap_kernel, grid=(edge_count // pair,), out_shape=jax.Sh...  4.98 us
    pallas_call x1, Pallas kernels, kernel_body(): pl.pallas_call(functools.partial(interpolate_kernel, capacity), out_shape...  2.9 us
    pallas_call x1, Pallas kernels, kernel_body(): pl.pallas_call(functools.partial(select_kernel, (edge_count, capacity, bl...  2.67 us
    unnamed x4, local copies, waits for them, and re-layouts  1.28 us
  transfers between devices with their start and end apart: 2, of which 1 were waited for; matrix products, arithmetic and copies ran while one was open for 0% of the time, Pallas kernels for 6%

profile of v1, /device:TPU:0, one launch (start us, length us, event | category | flops | bytes accessed | tf_op | source)
XLA Modules:
  0.0 47.1 jit_solution(17638545228076394745)
XLA Ops:
  0.0 0.5 collective-permute-start
  0.5 5.9 %collective-permute-start.1 = (bf16[1,450,128]{2,1,0:T(8,128)(2,1)}, bf16[1,450,128]{2,1,0:T(8,128)(2,1)S(1)}, u32[]{:S(2)}, u32[]{:S(2)}) collective-permute-start(bf16[1,450,128]{2,1,0:T(8,128)(2,1)} %own_ref.1), channel_id=1, source_target_pairs={{1,0},{2,1},{3,2},{4,3},{5,4},{6,5},{7,6},{8,7},{9,8},{10,9},{11,1... | collective-permute-start | bytes 345608 | tf_op jit(solution)/shard_map/ppermute | solution.py:19
  6.4 2.7 %select_weights.1.weight_ref = bf16[384,1024]{1,0:T(8,128)(2,1)} custom-call(s32[2,4]{1,0:T(2,128)} %bitcast.5, s32[4,128]{1,0:T(4,128)} %bitcast.4, bf16[4,2,128,128]{3,2,1,0:T(8,128)(2,1)} %weight_ref.1), custom_call_target="tpu_custom_call" | custom-call | flops 402653184 | bytes 786432 | tf_op jit(solution)/shard_map/select_weights/pallas_call | solution.py:103
  9.0 0.1 collective-permute-done.before_ref
  9.2 0.0 copy-start
  9.2 0.0 collective-permute-done.1.after_ref
  9.2 0.6 %copy-done = bf16[1,450,128]{2,1,0:T(8,128)(2,1)} copy-done((bf16[1,450,128]{2,1,0:T(8,128)(2,1)}, bf16[1,450,128]{2,1,0:T(8,128)(2,1)S(1)}, u32[]{:S(2)}) %copy-start) | copy-done | bytes 115224
  9.8 0.0 copy-start.1
  9.8 0.7 %copy-done.1 = bf16[1,450,128]{2,1,0:T(8,128)(2,1)} copy-done((bf16[1,450,128]{2,1,0:T(8,128)(2,1)}, bf16[1,450,128]{2,1,0:T(8,128)(2,1)S(1)}, u32[]{:S(2)}) %copy-start.1) | copy-done | bytes 115224
  10.4 2.9 %interpolate.1 = bf16[8,450,128]{2,1,0:T(8,128)(2,1)} custom-call(bf16[1,450,128]{2,1,0:T(8,128)(2,1)} %copy-done, bf16[1,450,128]{2,1,0:T(8,128)(2,1)} %own_ref.1, bf16[1,450,128]{2,1,0:T(8,128)(2,1)} %copy-done.1, bf16[384,1024]{1,0:T(8,128)(2,1)} %select_weights.1.weight_ref), custom_call_target="tpu_custom_call" | custom-call | flops 353894400 | bytes 921600 | tf_op jit(solution)/shard_map/interpolate/pallas_call | solution.py:116
  13.3 28.8 %all_to_all.5.inbox_ref = bf16[8,450,128]{2,1,0:T(8,128)(2,1)} all-to-all(bf16[8,450,128]{2,1,0:T(8,128)(2,1)} %interpolate.1), channel_id=1, replica_groups=mesh['side'=4,'edge'=8] {'edge'}, dimensions={0} | all-to-all | bytes 1843200 | tf_op jit(solution)/shard_map/all_to_all | solution.py:128
  42.1 5.0 %remap.1 = bf16[5,400,1024]{2,1,0:T(8,128)(2,1)} custom-call(bf16[8,450,128]{2,1,0:T(8,128)(2,1)} %all_to_all.5.inbox_ref, bf16[5,90,400]{2,1,0:T(8,128)(2,1)} %bitcast.3), custom_call_target="tpu_custom_call" | custom-call | flops 368640000 | bytes 4096000 | tf_op jit(solution)/shard_map/remap/pallas_call | solution.py:130
Async XLA Ops:
  0.0 9.2 %collective-permute-start = (bf16[1,450,128]{2,1,0:T(8,128)(2,1)}, bf16[1,450,128]{2,1,0:T(8,128)(2,1)S(1)}, u32[]{:S(2)}, u32[]{:S(2)}) collective-permute-start(bf16[1,450,128]{2,1,0:T(8,128)(2,1)} %own_ref.1), channel_id=1, source_target_pairs={{0,1},{1,2},{2,3},{3,4},{4,5},{5,6},{6,7},{7,8},{8,9},{9,10},{10,1... | collective-permute-start | bytes 345608 | tf_op jit(solution)/shard_map/ppermute | solution.py:19
  0.5 8.7 %collective-permute-start.1 = (bf16[1,450,128]{2,1,0:T(8,128)(2,1)}, bf16[1,450,128]{2,1,0:T(8,128)(2,1)S(1)}, u32[]{:S(2)}, u32[]{:S(2)}) collective-permute-start(bf16[1,450,128]{2,1,0:T(8,128)(2,1)} %own_ref.1), channel_id=1, source_target_pairs={{1,0},{2,1},{3,2},{4,3},{5,4},{6,5},{7,6},{8,7},{9,8},{10,9},{11,1... | collective-permute-start | bytes 345608 | tf_op jit(solution)/shard_map/ppermute | solution.py:19
  9.2 0.6 %copy-start = (bf16[1,450,128]{2,1,0:T(8,128)(2,1)}, bf16[1,450,128]{2,1,0:T(8,128)(2,1)S(1)}, u32[]{:S(2)}) copy-start(bf16[1,450,128]{2,1,0:T(8,128)(2,1)S(1)} %collective-permute-done.before_ref) | copy-start | bytes 345604
  9.8 0.7 %copy-start.1 = (bf16[1,450,128]{2,1,0:T(8,128)(2,1)}, bf16[1,450,128]{2,1,0:T(8,128)(2,1)S(1)}, u32[]{:S(2)}) copy-start(bf16[1,450,128]{2,1,0:T(8,128)(2,1)S(1)} %collective-permute-done.1.after_ref) | copy-start | bytes 345604

commit v2 on v1

--- a/solution.py
+++ b/solution.py
@@ -111,7 +111,7 @@
             bytes_accessed=2 * 3 * pcol * slots,
             transcendentals=0,
         ),
-        name="select_weights",
+        name="select_weights", compiler_params=pltpu.CompilerParams(vmem_limit_bytes=16 << 20),
     )(tile_source.T, destination.reshape(tiles, tile_rows), interp_weight)
     outbox = pl.pallas_call(
         functools.partial(interpolate_kernel, capacity),
@@ -123,7 +123,7 @@
             bytes_accessed=2 * features * slots,
             transcendentals=0,
         ),
-        name="interpolate",
+        name="interpolate", compiler_params=pltpu.CompilerParams(vmem_limit_bytes=16 << 20),
     )(before, parent_blocks, after, weights)
     inbox = lax.all_to_all(outbox, "edge", split_axis=0, concat_axis=0, tiled=True)
     pair = 2
@@ -141,7 +141,7 @@
             bytes_accessed=2 * variables * child_levels * slots,
             transcendentals=0,
         ),
-        name="remap",
+        name="remap", compiler_params=pltpu.CompilerParams(vmem_limit_bytes=16 << 20),
     )(inbox, jnp.swapaxes(remap_matrix, 1, 2))
 
 

time: 47.4 us -> 43.4 us (0.916)
  Pallas kernels: 10.5 us -> 5.34 us
  local copies, waits for them, and re-layouts: 1.28 us -> 3.21 us
  blocking collectives: 28.8 us -> 28.2 us
    pallas_call x1, Pallas kernels: 2.9 us -> 0.66 us  [kernel_body(): pl.pallas_call(functools.partial(interpolate_kernel, capacity), out_shape...]
    unnamed x4 -> x10, local copies, waits for them, and re-layouts: 1.28 us -> 3.21 us
    pallas_call x1, Pallas kernels: 4.98 us -> 3.33 us  [kernel_body(): pl.pallas_call(remap_kernel, grid=(edge_count // pair,), out_shape=jax.Sh...]
    pallas_call x1, Pallas kernels: 2.67 us -> 1.35 us  [kernel_body(): pl.pallas_call(functools.partial(select_kernel, (edge_count, capacity, bl...]
    all_to_all x1, blocking collectives: 28.8 us -> 28.2 us  [kernel_body(): lax.all_to_all(outbox, 'edge', split_axis=0, concat_axis=0, tiled=True)]
  transfers between devices with their start and end apart: 2 -> 2, of which waited for: 1 -> 0; matrix products, arithmetic and copies ran while one was open for 0% -> 0% of each run, Pallas kernels for 6% -> 3%
where the time goes in v2:
time: 43.4 us; the launch traced here: 43.2 us
  blocking collectives  28.2 us (65%)
  starting transfers between devices  6.42 us (15%)
  Pallas kernels  5.34 us (12%)
  local copies, waits for them, and re-layouts  3.21 us (7%)
    all_to_all x1, blocking collectives, kernel_body(): lax.all_to_all(outbox, 'edge', split_axis=0, concat_axis=0, tiled=True)  28.2 us
    ppermute x2, starting transfers between devices, neighbours(): return (lax.ppermute(block, AXES, up), lax.ppermute(block, AXES, down))  6.42 us
    pallas_call x1, Pallas kernels, kernel_body(): pl.pallas_call(remap_kernel, grid=(edge_count // pair,), out_shape=jax.Sh...  3.33 us
    unnamed x10, local copies, waits for them, and re-layouts  3.21 us
    pallas_call x1, Pallas kernels, kernel_body(): pl.pallas_call(functools.partial(select_kernel, (edge_count, capacity, bl...  1.35 us
  transfers between devices with their start and end apart: 2, of which 0 were waited for; matrix products, arithmetic and copies ran while one was open for 0% of the time, Pallas kernels for 3%

profile of v2, /device:TPU:0, one launch (start us, length us, event | category | flops | bytes accessed | tf_op | source)
XLA Modules:
  0.0 43.2 jit_solution(224332941659672679)
XLA Ops:
  0.0 0.0 copy-start
  0.0 0.5 %collective-permute-start = (bf16[1,450,128]{2,1,0:T(8,128)(2,1)}, bf16[1,450,128]{2,1,0:T(8,128)(2,1)S(1)}, u32[]{:S(2)}, u32[]{:S(2)}) collective-permute-start(bf16[1,450,128]{2,1,0:T(8,128)(2,1)} %own_ref.1), channel_id=1, source_target_pairs={{0,1},{1,2},{2,3},{3,4},{4,5},{5,6},{6,7},{7,8},{8,9},{9,10},{10,1... | collective-permute-start | bytes 345608 | tf_op jit(solution)/shard_map/ppermute | solution.py:19
  0.5 6.0 %collective-permute-start.1 = (bf16[1,450,128]{2,1,0:T(8,128)(2,1)}, bf16[1,450,128]{2,1,0:T(8,128)(2,1)S(1)}, u32[]{:S(2)}, u32[]{:S(2)}) collective-permute-start(bf16[1,450,128]{2,1,0:T(8,128)(2,1)} %own_ref.1), channel_id=1, source_target_pairs={{1,0},{2,1},{3,2},{4,3},{5,4},{6,5},{7,6},{8,7},{9,8},{10,9},{11,1... | collective-permute-start | bytes 345608 | tf_op jit(solution)/shard_map/ppermute | solution.py:19
  6.4 0.0 copy-start.2
  6.4 0.9 %copy-done.2 = bf16[4,2,128,128]{3,2,1,0:T(8,128)(2,1)S(1)} copy-done((bf16[4,2,128,128]{3,2,1,0:T(8,128)(2,1)S(1)}, bf16[4,2,128,128]{3,2,1,0:T(8,128)(2,1)}, u32[]{:S(2)}) %copy-start.2) | copy-done | bytes 262168
  7.4 0.0 copy-start.3
  7.4 0.7 %copy-done.3 = s32[512,1]{0,1:T(1,128)S(1)} copy-done((s32[512,1]{0,1:T(1,128)S(1)}, s32[512,1]{0,1:T(1,128)}, u32[]{:S(2)}) %copy-start.3) | copy-done | bytes 2072
  8.1 0.0 copy-start.4
  8.1 0.7 %copy-done.4 = s32[4,2]{0,1:T(2,128)S(1)} copy-done((s32[4,2]{0,1:T(2,128)S(1)}, s32[4,2]{0,1:T(2,128)}, u32[]{:S(2)}) %copy-start.4) | copy-done | bytes 56
  8.7 1.4 %select_weights.1.weight_ref = bf16[384,1024]{1,0:T(8,128)(2,1)S(1)} custom-call(s32[2,4]{1,0:T(2,128)S(1)} %bitcast.5, s32[4,128]{1,0:T(4,128)S(1)} %bitcast.4, bf16[4,2,128,128]{3,2,1,0:T(8,128)(2,1)S(1)} %copy-done.2), custom_call_target="tpu_custom_call" | custom-call | flops 402653184 | bytes 786432 | tf_op jit(solution)/shard_map/select_weights/pallas_call | solution.py:103
  10.1 0.0 collective-permute-done.before_ref
  10.1 0.0 collective-permute-done.1.after_ref
  10.1 0.0 copy-start.1
  10.1 0.9 %copy-done.1 = bf16[1,450,128]{2,1,0:T(8,128)(2,1)S(1)} copy-done((bf16[1,450,128]{2,1,0:T(8,128)(2,1)S(1)}, bf16[1,450,128]{2,1,0:T(8,128)(2,1)}, u32[]{:S(2)}) %copy-start.1) | copy-done | bytes 115224
  11.0 0.7 %interpolate.1 = bf16[8,450,128]{2,1,0:T(8,128)(2,1)S(1)} custom-call(bf16[1,450,128]{2,1,0:T(8,128)(2,1)S(1)} %collective-permute-done.before_ref, bf16[1,450,128]{2,1,0:T(8,128)(2,1)S(1)} %copy-done.1, bf16[1,450,128]{2,1,0:T(8,128)(2,1)S(1)} %collective-permute-done.1.after_ref, bf16[384,1024]{1,0:T(8,128)(2,1)S(1)} %select_weights.1.weight_ref), custom_call_target="tpu_custom_call" | custom-call | flops 353894400 | bytes 921600 | tf_op jit(solution)/shard_map/interpolate/pallas_call | solution.py:116
  11.7 28.2 %all_to_all.5.inbox_ref = bf16[8,450,128]{2,1,0:T(8,128)(2,1)S(1)} all-to-all(bf16[8,450,128]{2,1,0:T(8,128)(2,1)S(1)} %interpolate.1), channel_id=1, replica_groups=mesh['side'=4,'edge'=8] {'edge'}, dimensions={0} | all-to-all | bytes 1843200 | tf_op jit(solution)/shard_map/all_to_all | solution.py:128
  39.8 0.0 copy-done
  39.8 3.3 %remap.1 = bf16[5,400,1024]{2,1,0:T(8,128)(2,1)} custom-call(bf16[8,450,128]{2,1,0:T(8,128)(2,1)S(1)} %all_to_all.5.inbox_ref, bf16[5,90,400]{2,1,0:T(8,128)(2,1)S(1)} %bitcast.3), custom_call_target="tpu_custom_call" | custom-call | flops 368640000 | bytes 4096000 | tf_op jit(solution)/shard_map/remap/pallas_call | solution.py:130
Async XLA Ops:
  0.0 39.8 %copy-start = (bf16[5,400,90]{1,2,0:T(8,128)(2,1)S(1)}, bf16[5,400,90]{1,2,0:T(8,128)(2,1)}, u32[]{:S(2)}) copy-start(bf16[5,400,90]{1,2,0:T(8,128)(2,1)} %param.9) | copy-start | bytes 1080004
  0.0 10.1 %collective-permute-start = (bf16[1,450,128]{2,1,0:T(8,128)(2,1)}, bf16[1,450,128]{2,1,0:T(8,128)(2,1)S(1)}, u32[]{:S(2)}, u32[]{:S(2)}) collective-permute-start(bf16[1,450,128]{2,1,0:T(8,128)(2,1)} %own_ref.1), channel_id=1, source_target_pairs={{0,1},{1,2},{2,3},{3,4},{4,5},{5,6},{6,7},{7,8},{8,9},{9,10},{10,1... | collective-permute-start | bytes 345608 | tf_op jit(solution)/shard_map/ppermute | solution.py:19
  0.5 9.7 %collective-permute-start.1 = (bf16[1,450,128]{2,1,0:T(8,128)(2,1)}, bf16[1,450,128]{2,1,0:T(8,128)(2,1)S(1)}, u32[]{:S(2)}, u32[]{:S(2)}) collective-permute-start(bf16[1,450,128]{2,1,0:T(8,128)(2,1)} %own_ref.1), channel_id=1, source_target_pairs={{1,0},{2,1},{3,2},{4,3},{5,4},{6,5},{7,6},{8,7},{9,8},{10,9},{11,1... | collective-permute-start | bytes 345608 | tf_op jit(solution)/shard_map/ppermute | solution.py:19
  6.4 0.9 %copy-start.2 = (bf16[4,2,128,128]{3,2,1,0:T(8,128)(2,1)S(1)}, bf16[4,2,128,128]{3,2,1,0:T(8,128)(2,1)}, u32[]{:S(2)}) copy-start(bf16[4,2,128,128]{3,2,1,0:T(8,128)(2,1)} %weight_ref.1) | copy-start | bytes 786436
  7.4 0.7 %copy-start.3 = (s32[512,1]{0,1:T(1,128)S(1)}, s32[512,1]{0,1:T(1,128)}, u32[]{:S(2)}) copy-start(s32[512,1]{0,1:T(1,128)} %param.8) | copy-start | bytes 6148
  8.1 0.7 %copy-start.4 = (s32[4,2]{0,1:T(2,128)S(1)}, s32[4,2]{0,1:T(2,128)}, u32[]{:S(2)}) copy-start(s32[4,2]{0,1:T(2,128)} %param.7) | copy-start | bytes 100
  10.1 0.9 %copy-start.1 = (bf16[1,450,128]{2,1,0:T(8,128)(2,1)S(1)}, bf16[1,450,128]{2,1,0:T(8,128)(2,1)}, u32[]{:S(2)}) copy-start(bf16[1,450,128]{2,1,0:T(8,128)(2,1)} %own_ref.1) | copy-start | bytes 345604

commit v3 on v1

v3 whole, which is shorter than its diff:
```python
import functools

import jax
import jax.numpy as jnp
from jax import lax
from jax.experimental import pallas as pl
from jax.experimental.pallas import tpu as pltpu
from jax.sharding import PartitionSpec as P

AXES = ("side", "edge")
VMEM = pl.BlockSpec(memory_space=pltpu.VMEM)
HBM = pl.BlockSpec(memory_space=pltpu.HBM)
ROOM = pltpu.CompilerParams(vmem_limit_bytes=20 << 20)
WINDOW = 112


def neighbours(block):
    count = lax.axis_size(AXES)
    up = [(i, (i + 1) % count) for i in range(count)]
    down = [(j, i) for i, j in up]
    return lax.ppermute(block, AXES, up), lax.ppermute(block, AXES, down)


def slot_rows(owner_count, capacity, dest):
    tiles, lanes = dest.shape
    owner = lax.broadcasted_iota(jnp.int32, (owner_count, lanes), 0)
    hits = [(dest[t : t + 1, :] == owner).astype(jnp.float32) for t in range(tiles)]
    earlier = (
        lax.broadcasted_iota(jnp.int32, (lanes, lanes), 0)
        < lax.broadcasted_iota(jnp.int32, (lanes, lanes), 1)
    ).astype(jnp.bfloat16)
    stacked = jnp.concatenate(hits, axis=0).astype(jnp.bfloat16)
    before = jnp.dot(stacked, earlier, preferred_element_type=jnp.float32)
    carry = jnp.zeros((owner_count, 1), jnp.float32)
    slots = []
    for t in range(tiles):
        place = before[t * owner_count : (t + 1) * owner_count, :] + carry
        rank = jnp.sum(hits[t] * place, axis=0, keepdims=True)
        slots.append(dest[t : t + 1, :] * capacity + rank.astype(jnp.int32))
        carry = carry + jnp.sum(hits[t], axis=1, keepdims=True)
    return slots


def window_of(v, levels):
    first = v * levels // 16 * 16
    return first, v * levels - first


def select_kernel(sizes, source_hbm, dest_hbm, weight_hbm, out_ref, source, dest, weight, spread, sems):
    owner_count, capacity, block_count = sizes
    tiles, _, pcol, rows = weight.shape
    copies = [
        pltpu.make_async_copy(a, b, sems.at[i])
        for i, (a, b) in enumerate([(dest_hbm, dest), (source_hbm, source), (weight_hbm, weight)])
    ]
    for copy in copies:
        copy.start()
    position = lax.axis_index("side") * owner_count + lax.axis_index("edge")
    copies[0].wait()
    slots = slot_rows(owner_count, capacity, dest[...])
    copies[1].wait()
    copies[2].wait()
    for t in range(tiles):
        first, second = (
            lax.rem(source[k, t] - position + 1 + block_count, block_count) for k in range(2)
        )
        swapped = (first > second).astype(jnp.int32)
        lanes = slice(t * rows, (t + 1) * rows)
        spread[0:pcol, lanes] = weight[t, swapped]
        spread[pcol : 2 * pcol, lanes] = weight[t, 1 - swapped]
        left_out = jnp.full((16, rows), 3 - first - second, jnp.int32)
        spread[2 * pcol : 2 * pcol + 16, lanes] = left_out.astype(jnp.float32).astype(jnp.bfloat16)
    pair = 2
    width = pair * capacity
    height = out_ref.shape[1]
    for c in range(owner_count // pair):
        slot = lax.broadcasted_iota(jnp.int32, (width, rows), 0) + c * width
        chosen = jnp.concatenate(
            [(slot == slots[t]).astype(jnp.float32).astype(jnp.bfloat16) for t in range(tiles)],
            axis=1,
        )
        picked = lax.dot_general(
            spread[...], chosen, (((1,), (1,)), ((), ())), preferred_element_type=jnp.float32
        ).astype(jnp.bfloat16)
        for i in range(pair):
            out_ref[c * pair + i] = picked[:height, i * capacity : (i + 1) * capacity]


def lay_remap_kernel(remap_ref, out_ref):
    variables, levels, child_levels = remap_ref.shape
    for v in range(variables):
        _, place = window_of(v, levels)
        parts = [remap_ref[v].astype(jnp.float32)]
        if place:
            parts.insert(0, jnp.zeros((place, child_levels), jnp.float32))
        parts.append(jnp.zeros((128 - place - levels, child_levels), jnp.float32))
        turned = jnp.concatenate(parts, axis=0).T
        out_ref[v] = turned[:, :WINDOW].astype(jnp.bfloat16)


def join_kernel(own_ref, other_ref, weight_ref, remap_ref, out_ref):
    out_ref[0] = own_ref[0]
    out_ref[1] = other_ref[0]


def collect_kernel(joined_ref, near_ref, held_ref, rim_ref):
    edge = lax.axis_index("edge")
    place, core = edge // 2, lax.rem(edge, 2)
    held_ref[0] = joined_ref[0]
    held_ref[1] = near_ref[0]
    held_ref[2] = joined_ref[1]
    held_ref[3] = near_ref[1]
    rim_ref[0] = held_ref[jnp.bitwise_xor(place, 3 * core)]


def finish_kernel(
    inbox_ref, held_ref, rim_ref, other_ref, other_rim_ref, remap_ref, out_hbm, coarse, result, sems
):
    edge = lax.axis_index("edge")
    place, core = edge // 2, lax.rem(edge, 2)
    variables, child_levels, _ = remap_ref.shape
    features = held_ref.shape[1]
    levels = features // variables
    pcol = held_ref.shape[2]
    capacity = inbox_ref.shape[2]
    chips = inbox_ref.shape[0] // 2

    def block(chip, parity):
        inside = jnp.logical_and(chip >= 0, chip < chips)
        where = jnp.bitwise_and(jnp.bitwise_xor(chip, place), chips - 1)
        mine = jnp.where(inside, held_ref[where], rim_ref[0])
        theirs = jnp.where(inside, other_ref[where], other_rim_ref[0])
        return jnp.where(core == parity, mine, theirs)

    copies = []
    for step in range(chips):
        chip = jnp.bitwise_xor(place, step)
        parents = jnp.concatenate(
            [block(chip - 1, 1), block(chip, 0), block(chip, 1), block(chip + 1, 0)], axis=1
        )
        columns = []
        for parity in range(2):
            sent = inbox_ref.at[2 * chip + parity]
            low, high = sent[0:pcol, :], sent[pcol : 2 * pcol, :]
            left_out = jnp.broadcast_to(sent[2 * pcol : 2 * pcol + 1, :].astype(jnp.float32), (pcol, capacity))
            zero = jnp.zeros_like(low)
            parts = [
                jnp.where(left_out > 0.5, low, zero),
                jnp.where(left_out < 0.5, low, jnp.where(left_out > 1.5, high, zero)),
                jnp.where(left_out < 1.5, high, zero),
            ]
            parts.insert(3 if parity == 0 else 0, zero)
            columns.append(jnp.concatenate(parts, axis=0))
        coarse[step, 0:features, :] = jnp.dot(
            parents, jnp.concatenate(columns, axis=1), preferred_element_type=jnp.float32
        ).astype(jnp.bfloat16)
        rest = coarse.shape[1] - features
        coarse[step, features:, :] = jnp.zeros((rest, 2 * capacity), jnp.bfloat16)
        for v in range(variables):
            first, _ = window_of(v, levels)
            result[step, v] = jnp.dot(
                remap_ref[v],
                coarse[step, first : first + WINDOW, :],
                preferred_element_type=jnp.float32,
            ).astype(jnp.bfloat16)
            slots = pl.ds(pl.multiple_of(chip * 2 * capacity, 2 * capacity), 2 * capacity)
            copy = pltpu.make_async_copy(result.at[step, v], out_hbm.at[v, :, slots], sems.at[step, v])
            copy.start()
            copies.append(copy)
    for copy in copies:
        copy.wait()


def exchange(array, distance):
    count = lax.axis_size("edge")
    return lax.ppermute(array, "edge", [(i, i ^ distance) for i in range(count)])


def across_sides(array):
    sides, count = lax.axis_size("side"), lax.axis_size("edge")
    moves = [
        (s * count + e, (s + (1 if e % 2 else -1)) % sides * count + e)
        for s in range(sides)
        for e in range(count)
    ]
    return lax.ppermute(array, AXES, moves)


def kernel_body(parent_blocks, interp_weight, tile_source, destination, remap_matrix):
    edge_count = lax.axis_size("edge")
    block_count = lax.axis_size(AXES)
    tiles, _, pcol, tile_rows = interp_weight.shape
    features = parent_blocks.shape[1]
    variables, child_levels, levels = remap_matrix.shape
    capacity = 2 * destination.shape[0] // edge_count
    slots = edge_count * capacity
    chips = edge_count // 2
    bf16 = jnp.bfloat16

    def cost(flops, bytes_accessed):
        return pl.CostEstimate(flops=flops, bytes_accessed=bytes_accessed, transcendentals=0)

    far = exchange(parent_blocks, 4)
    height = 2 * pcol + 8
    outbox = pl.pallas_call(
        functools.partial(select_kernel, (edge_count, capacity, block_count)),
        out_shape=jax.ShapeDtypeStruct((edge_count, height, capacity), bf16),
        in_specs=[HBM, HBM, HBM],
        out_specs=VMEM,
        scratch_shapes=[
            pltpu.SMEM((2, tiles), jnp.int32),
            pltpu.VMEM((tiles, tile_rows), jnp.int32),
            pltpu.VMEM(interp_weight.shape, bf16),
            pltpu.VMEM((2 * pcol + 16, tiles * tile_rows), bf16),
            pltpu.SemaphoreType.DMA((3,)),
        ],
        cost_estimate=cost(2 * height * tiles * tile_rows * slots, 2 * height * slots),
        compiler_params=ROOM,
        name="select_weights",
    )(tile_source.T, destination.reshape(tiles, tile_rows), interp_weight)
    inbox = lax.all_to_all(outbox, "edge", split_axis=0, concat_axis=0, tiled=True)
    laid = pl.pallas_call(
        lay_remap_kernel,
        out_shape=jax.ShapeDtypeStruct((variables, child_levels, WINDOW), bf16),
        in_specs=[VMEM],
        out_specs=VMEM,
        compiler_params=ROOM,
        cost_estimate=cost(0, 4 * variables * child_levels * levels),
        name="lay_remap",
    )(jnp.swapaxes(remap_matrix, 1, 2))
    block_bytes = 2 * features * pcol
    joined = pl.pallas_call(
        join_kernel,
        out_shape=jax.ShapeDtypeStruct((2, features, pcol), bf16),
        in_specs=[VMEM, VMEM, pl.BlockSpec(memory_space=pl.ANY), pl.BlockSpec(memory_space=pl.ANY)],
        out_specs=VMEM,
        compiler_params=ROOM,
        cost_estimate=cost(0, 4 * block_bytes),
        name="join",
    )(parent_blocks, far, outbox, laid)
    near = exchange(joined, 2)
    held, rim = pl.pallas_call(
        collect_kernel,
        out_shape=(
            jax.ShapeDtypeStruct((chips, features, pcol), bf16),
            jax.ShapeDtypeStruct((1, features, pcol), bf16),
        ),
        in_specs=[VMEM, VMEM],
        out_specs=(VMEM, VMEM),
        compiler_params=ROOM,
        cost_estimate=cost(0, 9 * block_bytes),
        name="collect",
    )(joined, near)
    rim = across_sides(rim)
    other = exchange(held, 1)
    other_rim = exchange(rim, 1)
    return pl.pallas_call(
        finish_kernel,
        out_shape=jax.ShapeDtypeStruct((variables, child_levels, slots), bf16),
        in_specs=[VMEM] * 6,
        out_specs=HBM,
        scratch_shapes=[
            pltpu.VMEM((chips, 464, 2 * capacity), bf16),
            pltpu.VMEM((chips, variables, child_levels, 2 * capacity), bf16),
            pltpu.SemaphoreType.DMA((chips, variables)),
        ],
        compiler_params=ROOM,
        cost_estimate=cost(
            2 * slots * (4 * pcol * features + variables * child_levels * levels),
            2 * variables * child_levels * slots,
        ),
        name="finish",
    )(inbox, held, rim, other, other_rim, laid)


def plain_body(parent_blocks, interp_weight, tile_source, destination, remap_matrix):
    edge_count = lax.axis_size("edge")
    block_count = lax.axis_size(AXES)
    position = lax.axis_index(AXES)
    before, after = neighbours(parent_blocks)
    rim_blocks = jnp.concatenate([before, parent_blocks, after], axis=0)
    offset = (tile_source - position + 1 + block_count) % block_count
    chosen = rim_blocks[offset]
    summed = jnp.einsum(
        "tkfp,tkpr->tfr", chosen, interp_weight, preferred_element_type=jnp.float32
    )
    coarse = summed.astype(jnp.bfloat16)
    tile_count, feat_count, tile_rows = coarse.shape
    rows = coarse.transpose(1, 0, 2).reshape(feat_count, tile_count * tile_rows)
    row_count = destination.shape[0]
    capacity = max(2, 2 * row_count // edge_count)
    owners = destination[:, 0]
    owner_hits = (owners[:, None] == jnp.arange(edge_count, dtype=jnp.int32)[None, :]).astype(
        jnp.int32
    )
    places = jnp.sum(jnp.cumsum(owner_hits, axis=0) * owner_hits, axis=1) - 1
    slot_index = owners * capacity + places
    outbox = (
        jnp.zeros((feat_count, edge_count * capacity), jnp.bfloat16).at[:, slot_index].set(rows)
    )
    inbox = lax.all_to_all(outbox, "edge", split_axis=1, concat_axis=1, tiled=True)
    shaped = inbox.reshape(remap_matrix.shape[0], remap_matrix.shape[2], inbox.shape[1])
    result = jnp.einsum("vcl,vln->vcn", remap_matrix, shaped, preferred_element_type=jnp.float32)
    return result.astype(jnp.bfloat16)


def solution(mesh):
    body = kernel_body if mesh.shape["edge"] == 8 else plain_body
    return jax.shard_map(
        body,
        mesh=mesh,
        in_specs=(
            P(AXES, None, None),
            P(AXES, None, None, None),
            P(AXES, None),
            P(AXES, None),
            P(),
        ),
        out_specs=P(None, None, AXES),
        check_vma=False,
    )
```

time: 47.4 us -> 50.6 us (1.068)
  blocking collectives: 28.8 us -> 0 us
  waiting for transfers between devices: 0.11 us -> 28.3 us
  starting transfers between devices: 6.37 us -> 11.9 us
  Pallas kernels: 10.5 us -> 5.7 us
  local copies, waits for them, and re-layouts: 1.28 us -> 4.24 us
    all_to_all x1 -> x0, blocking collectives: 28.8 us -> none  [kernel_body(): lax.all_to_all(outbox, 'edge', split_axis=0, concat_axis=0, tiled=True)]
    ppermute x2 -> x5, waiting for transfers between devices: 0.11 us -> 28.3 us  [the longest x4 25.1 us: exchange(): lax.ppermute(array, 'edge', [(i, i ^ distance) for i in range(count)])]
    all_to_all x0 -> x1, starting transfers between devices: none -> 6.34 us  [kernel_body(): lax.all_to_all(outbox, 'edge', split_axis=0, concat_axis=0, tiled=True)]
    pallas_call x2 -> x4, Pallas kernels: 7.88 us -> 3.82 us  [the longest x1 3.53 us: kernel_body(): pl.pallas_call(finish_kernel, out_shape=jax.ShapeDtypeStruct((variables,...]
    unnamed x4 -> x10, local copies, waits for them, and re-layouts: 1.28 us -> 4.24 us
    pallas_call x1, Pallas kernels: 2.67 us -> 1.88 us  [kernel_body(): pl.pallas_call(functools.partial(select_kernel, (edge_count, capacity, bl...]
    ppermute x2 -> x5, starting transfers between devices: 6.37 us -> 5.58 us  [the longest x4 3.08 us: exchange(): lax.ppermute(array, 'edge', [(i, i ^ distance) for i in range(count)])]
  transfers between devices with their start and end apart: 2 -> 6, of which waited for: 1 -> 4; matrix products, arithmetic and copies ran while one was open for 0% -> 0% of each run, Pallas kernels for 6% -> 1%
where the time goes in v3:
time: 50.6 us; the launch traced here: 50.2 us
  waiting for transfers between devices  28.3 us (56%)
  starting transfers between devices  11.9 us (24%)
  Pallas kernels  5.7 us (11%)
  local copies, waits for them, and re-layouts  4.24 us (8%)
    ppermute x4, waiting for transfers between devices, exchange(): lax.ppermute(array, 'edge', [(i, i ^ distance) for i in range(count)])  25.1 us
    all_to_all x1, starting transfers between devices, kernel_body(): lax.all_to_all(outbox, 'edge', split_axis=0, concat_axis=0, tiled=True)  6.34 us
    unnamed x10, local copies, waits for them, and re-layouts  4.24 us
    pallas_call x1, Pallas kernels, kernel_body(): pl.pallas_call(finish_kernel, out_shape=jax.ShapeDtypeStruct((variables,...  3.53 us
    ppermute x1, waiting for transfers between devices, across_sides(): return lax.ppermute(array, AXES, moves)  3.27 us
    ppermute x4, starting transfers between devices, exchange(): lax.ppermute(array, 'edge', [(i, i ^ distance) for i in range(count)])  3.08 us
    ppermute x1, starting transfers between devices, across_sides(): return lax.ppermute(array, AXES, moves)  2.5 us
    pallas_call x1, Pallas kernels, kernel_body(): pl.pallas_call(functools.partial(select_kernel, (edge_count, capacity, bl...  1.88 us
  transfers between devices with their start and end apart: 6, of which 4 were waited for; matrix products, arithmetic and copies ran while one was open for 0% of the time, Pallas kernels for 1%

profile of v3, /device:TPU:0, one launch (start us, length us, event | category | flops | bytes accessed | tf_op | source)
XLA Modules:
  0.0 50.2 jit_solution(18071302798377776477)
XLA Ops:
  0.0 0.0 copy-start.2
  0.0 0.9 %copy-done.2 = bf16[4,2,128,128]{3,2,1,0:T(8,128)(2,1)S(1)} copy-done((bf16[4,2,128,128]{3,2,1,0:T(8,128)(2,1)S(1)}, bf16[4,2,128,128]{3,2,1,0:T(8,128)(2,1)}, u32[]{:S(2)}) %copy-start.2) | copy-done | bytes 262168
  1.0 0.0 copy-start.3
  1.0 0.7 %copy-done.3 = s32[512,1]{0,1:T(1,128)S(1)} copy-done((s32[512,1]{0,1:T(1,128)S(1)}, s32[512,1]{0,1:T(1,128)}, u32[]{:S(2)}) %copy-start.3) | copy-done | bytes 2072
  1.6 0.0 copy-start.4
  1.6 0.7 %copy-done.4 = s32[4,2]{0,1:T(2,128)S(1)} copy-done((s32[4,2]{0,1:T(2,128)S(1)}, s32[4,2]{0,1:T(2,128)}, u32[]{:S(2)}) %copy-start.4) | copy-done | bytes 56
  2.3 1.9 %select_weights.1.weight_ref = bf16[8,264,128]{2,1,0:T(8,128)(2,1)} custom-call(s32[2,4]{1,0:T(2,128)S(1)} %bitcast.5, s32[4,128]{1,0:T(4,128)S(1)} %bitcast.4, bf16[4,2,128,128]{3,2,1,0:T(8,128)(2,1)S(1)} %copy-done.2), custom_call_target="tpu_custom_call" | custom-call | flops 276824064 | bytes 540672 | tf_op jit(solution)/shard_map/select_weights/pallas_call | solution.py:205
  4.2 6.3 %all-to-all-start = ((bf16[8,264,128]{2,1,0:T(8,128)(2,1)}), bf16[8,264,128]{2,1,0:T(8,128)(2,1)S(1)}, u32[]{:S(2)}, u32[]{:S(2)}) async-start(bf16[8,264,128]{2,1,0:T(8,128)(2,1)} %select_weights.1.weight_ref), calls=%async_computation | async-start | bytes 1081344 | tf_op jit(solution)/shard_map/all_to_all | solution.py:221
  10.5 2.9 %collective-permute-start = (bf16[1,450,128]{2,1,0:T(8,128)(2,1)}, bf16[1,450,128]{2,1,0:T(8,128)(2,1)S(1)}, u32[]{:S(2)}, u32[]{:S(2)}) collective-permute-start(bf16[1,450,128]{2,1,0:T(8,128)(2,1)} %own_ref.1), channel_id=1, source_target_pairs={{0,4},{1,5},{2,6},{3,7},{4,0},{5,1},{6,2},{7,3},{8,12},{9,13},{10,... | collective-permute-start | bytes 345608 | tf_op jit(solution)/shard_map/ppermute | solution.py:176
  13.5 0.0 copy-start
  13.5 1.0 %copy-done = bf16[5,400,90]{1,2,0:T(8,128)(2,1)S(1)} copy-done((bf16[5,400,90]{1,2,0:T(8,128)(2,1)S(1)}, bf16[5,400,90]{1,2,0:T(8,128)(2,1)}, u32[]{:S(2)}) %copy-start) | copy-done | bytes 360024
  14.5 0.2 lay_remap.1.remap_ref
  14.7 16.5 %collective-permute-done.other_ref = bf16[1,450,128]{2,1,0:T(8,128)(2,1)S(1)} collective-permute-done((bf16[1,450,128]{2,1,0:T(8,128)(2,1)}, bf16[1,450,128]{2,1,0:T(8,128)(2,1)S(1)}, u32[]{:S(2)}, u32[]{:S(2)}) %collective-permute-start) | collective-permute-done | bytes 115232 | tf_op jit(solution)/shard_map/ppermute | solution.py:176
  31.3 0.0 copy-start.1
  31.3 0.9 %copy-done.1 = bf16[1,450,128]{2,1,0:T(8,128)(2,1)S(1)} copy-done((bf16[1,450,128]{2,1,0:T(8,128)(2,1)S(1)}, bf16[1,450,128]{2,1,0:T(8,128)(2,1)}, u32[]{:S(2)}) %copy-start.1) | copy-done | bytes 115224
  32.2 0.1 collective-permute-start.1
  32.3 7.2 %collective-permute-done.1.near_ref = bf16[2,450,128]{2,1,0:T(8,128)(2,1)S(1)} collective-permute-done((bf16[2,450,128]{2,1,0:T(8,128)(2,1)S(1)}, bf16[2,450,128]{2,1,0:T(8,128)(2,1)S(1)}, u32[]{:S(2)}, u32[]{:S(2)}) %collective-permute-start.1) | collective-permute-done | bytes 230432 | tf_op jit(solution)/shard_map/ppermute | solution.py:176
  39.5 0.1 collective-permute-start.3
  39.6 2.5 %collective-permute-start.2 = (bf16[1,450,128]{2,1,0:T(8,128)(2,1)S(1)}, bf16[1,450,128]{2,1,0:T(8,128)(2,1)S(1)}, u32[]{:S(2)}, u32[]{:S(2)}) collective-permute-start(bf16[1,450,128]{2,1,0:T(8,128)(2,1)S(1)} %get-tuple-element.8), channel_id=1, source_target_pairs={{0,24},{1,9},{2,26},{3,11},{4,28},{5,13},{6,30},{7,15},{8,0},{9,17... | collective-permute-start | bytes 345608 | tf_op jit(solution)/shard_map/ppermute | solution.py:186
  42.1 3.3 %collective-permute-done.2.rim_ref = bf16[1,450,128]{2,1,0:T(8,128)(2,1)S(1)} collective-permute-done((bf16[1,450,128]{2,1,0:T(8,128)(2,1)S(1)}, bf16[1,450,128]{2,1,0:T(8,128)(2,1)S(1)}, u32[]{:S(2)}, u32[]{:S(2)}) %collective-permute-start.2) | collective-permute-done | bytes 115232 | tf_op jit(solution)/shard_map/ppermute | solution.py:186
  45.4 0.0 collective-permute-start.4
  45.4 1.3 %collective-permute-done.4.other_rim_ref = bf16[1,450,128]{2,1,0:T(8,128)(2,1)S(1)} collective-permute-done((bf16[1,450,128]{2,1,0:T(8,128)(2,1)S(1)}, bf16[1,450,128]{2,1,0:T(8,128)(2,1)S(1)}, u32[]{:S(2)}, u32[]{:S(2)}) %collective-permute-start.4) | collective-permute-done | bytes 115232 | tf_op jit(solution)/shard_map/ppermute | solution.py:176
  46.7 0.0 collective-permute-done.3.other_ref
  46.7 0.0 all-to-all-done.inbox_ref
  46.7 3.5 %finish.1 = bf16[5,400,1024]{2,1,0:T(8,128)(2,1)} custom-call(bf16[8,264,128]{2,1,0:T(8,128)(2,1)S(1)} %all-to-all-done.inbox_ref, bf16[4,450,128]{2,1,0:T(8,128)(2,1)S(1)} %get-tuple-element.7.held_ref, bf16[1,450,128]{2,1,0:T(8,128)(2,1)S(1)} %collective-permute-done.2.rim_ref, bf16[4,450,128]{2,1,0:T(8,128)(2,1)S(1)} %collective-permute-done.3.other_ref, ...), custom_call_target="tpu_custom_call" | custom-call | flops 840499200 | bytes 4096000 | tf_op jit(solution)/shard_map/finish/pallas_call | solution.py:257
  (2 shorter events, 0.1 us)
Async XLA Ops:
  0.0 0.9 %copy-start.2 = (bf16[4,2,128,128]{3,2,1,0:T(8,128)(2,1)S(1)}, bf16[4,2,128,128]{3,2,1,0:T(8,128)(2,1)}, u32[]{:S(2)}) copy-start(bf16[4,2,128,128]{3,2,1,0:T(8,128)(2,1)} %weight_hbm.1) | copy-start | bytes 786436
  1.0 0.7 %copy-start.3 = (s32[512,1]{0,1:T(1,128)S(1)}, s32[512,1]{0,1:T(1,128)}, u32[]{:S(2)}) copy-start(s32[512,1]{0,1:T(1,128)} %param.8) | copy-start | bytes 6148
  1.6 0.7 %copy-start.4 = (s32[4,2]{0,1:T(2,128)S(1)}, s32[4,2]{0,1:T(2,128)}, u32[]{:S(2)}) copy-start(s32[4,2]{0,1:T(2,128)} %param.7) | copy-start | bytes 100
  4.2 42.5 %all-to-all-start = ((bf16[8,264,128]{2,1,0:T(8,128)(2,1)}), bf16[8,264,128]{2,1,0:T(8,128)(2,1)S(1)}, u32[]{:S(2)}, u32[]{:S(2)}) async-start(bf16[8,264,128]{2,1,0:T(8,128)(2,1)} %select_weights.1.weight_ref), calls=%async_computation | async-start | bytes 1081344 | tf_op jit(solution)/shard_map/all_to_all | solution.py:221
  10.5 20.7 %collective-permute-start = (bf16[1,450,128]{2,1,0:T(8,128)(2,1)}, bf16[1,450,128]{2,1,0:T(8,128)(2,1)S(1)}, u32[]{:S(2)}, u32[]{:S(2)}) collective-permute-start(bf16[1,450,128]{2,1,0:T(8,128)(2,1)} %own_ref.1), channel_id=1, source_target_pairs={{0,4},{1,5},{2,6},{3,7},{4,0},{5,1},{6,2},{7,3},{8,12},{9,13},{10,... | collective-permute-start | bytes 345608 | tf_op jit(solution)/shard_map/ppermute | solution.py:176
  13.5 1.0 %copy-start = (bf16[5,400,90]{1,2,0:T(8,128)(2,1)S(1)}, bf16[5,400,90]{1,2,0:T(8,128)(2,1)}, u32[]{:S(2)}) copy-start(bf16[5,400,90]{1,2,0:T(8,128)(2,1)} %param.9) | copy-start | bytes 1080004
  31.3 0.9 %copy-start.1 = (bf16[1,450,128]{2,1,0:T(8,128)(2,1)S(1)}, bf16[1,450,128]{2,1,0:T(8,128)(2,1)}, u32[]{:S(2)}) copy-start(bf16[1,450,128]{2,1,0:T(8,128)(2,1)} %own_ref.1) | copy-start | bytes 345604
  32.2 7.3 %collective-permute-start.1 = (bf16[2,450,128]{2,1,0:T(8,128)(2,1)S(1)}, bf16[2,450,128]{2,1,0:T(8,128)(2,1)S(1)}, u32[]{:S(2)}, u32[]{:S(2)}) collective-permute-start(bf16[2,450,128]{2,1,0:T(8,128)(2,1)S(1)} %join.1.joined_ref), channel_id=1, source_target_pairs={{0,2},{1,3},{2,0},{3,1},{4,6},{5,7},{6,4},{7,5},{8,10},{9,11},{10,... | collective-permute-start | bytes 691208 | tf_op jit(solution)/shard_map/ppermute | solution.py:176
  39.5 7.2 %collective-permute-start.3 = (bf16[4,450,128]{2,1,0:T(8,128)(2,1)S(1)}, bf16[4,450,128]{2,1,0:T(8,128)(2,1)S(1)}, u32[]{:S(2)}, u32[]{:S(2)}) collective-permute-start(bf16[4,450,128]{2,1,0:T(8,128)(2,1)S(1)} %get-tuple-element.7.held_ref), channel_id=1, source_target_pairs={{0,1},{1,0},{2,3},{3,2},{4,5},{5,4},{6,7},{7,6},{8,9},{9,8},{10,11... | collective-permute-start | bytes 1382408 | tf_op jit(solution)/shard_map/ppermute | solution.py:176
  39.6 5.8 %collective-permute-start.2 = (bf16[1,450,128]{2,1,0:T(8,128)(2,1)S(1)}, bf16[1,450,128]{2,1,0:T(8,128)(2,1)S(1)}, u32[]{:S(2)}, u32[]{:S(2)}) collective-permute-start(bf16[1,450,128]{2,1,0:T(8,128)(2,1)S(1)} %get-tuple-element.8), channel_id=1, source_target_pairs={{0,24},{1,9},{2,26},{3,11},{4,28},{5,13},{6,30},{7,15},{8,0},{9,17... | collective-permute-start | bytes 345608 | tf_op jit(solution)/shard_map/ppermute | solution.py:186
  45.4 1.3 %collective-permute-start.4 = (bf16[1,450,128]{2,1,0:T(8,128)(2,1)S(1)}, bf16[1,450,128]{2,1,0:T(8,128)(2,1)S(1)}, u32[]{:S(2)}, u32[]{:S(2)}) collective-permute-start(bf16[1,450,128]{2,1,0:T(8,128)(2,1)S(1)} %collective-permute-done.2.rim_ref), channel_id=1, source_target_pairs={{0,1},{1,0},{2,3},{3,2},{4,5},{5,4},{6,7},{7,6},{8,9},{9,8},{10,11... | collective-permute-start | bytes 345608 | tf_op jit(solution)/shard_map/ppermute | solution.py:176

commit v4 on v3

--- a/solution.py
+++ b/solution.py
@@ -10,6 +10,7 @@
 AXES = ("side", "edge")
 VMEM = pl.BlockSpec(memory_space=pltpu.VMEM)
 HBM = pl.BlockSpec(memory_space=pltpu.HBM)
+ANY = pl.BlockSpec(memory_space=pl.ANY)
 ROOM = pltpu.CompilerParams(vmem_limit_bytes=20 << 20)
 WINDOW = 112
 
@@ -98,9 +99,17 @@
         out_ref[v] = turned[:, :WINDOW].astype(jnp.bfloat16)
 
 
-def join_kernel(own_ref, other_ref, weight_ref, remap_ref, out_ref):
+def open_join_kernel(own_ref, out_ref):
     out_ref[0] = own_ref[0]
+
+
+def join_kernel(other_ref, half_ref, out_ref):
+    out_ref[0] = half_ref[0]
     out_ref[1] = other_ref[0]
+
+
+def pass_kernel(laid_ref, joined_ref, out_ref):
+    del laid_ref, joined_ref, out_ref
 
 
 def collect_kernel(joined_ref, near_ref, held_ref, rim_ref):
@@ -215,10 +224,9 @@
             pltpu.SemaphoreType.DMA((3,)),
         ],
         cost_estimate=cost(2 * height * tiles * tile_rows * slots, 2 * height * slots),
-        compiler_params=ROOM,
         name="select_weights",
     )(tile_source.T, destination.reshape(tiles, tile_rows), interp_weight)
-    inbox = lax.all_to_all(outbox, "edge", split_axis=0, concat_axis=0, tiled=True)
+    block_bytes = 2 * features * pcol
     laid = pl.pallas_call(
         lay_remap_kernel,
         out_shape=jax.ShapeDtypeStruct((variables, child_levels, WINDOW), bf16),
@@ -228,17 +236,37 @@
         cost_estimate=cost(0, 4 * variables * child_levels * levels),
         name="lay_remap",
     )(jnp.swapaxes(remap_matrix, 1, 2))
-    block_bytes = 2 * features * pcol
+    half = pl.pallas_call(
+        open_join_kernel,
+        out_shape=jax.ShapeDtypeStruct((2, features, pcol), bf16),
+        in_specs=[VMEM],
+        out_specs=VMEM,
+        compiler_params=ROOM,
+        cost_estimate=cost(0, 4 * block_bytes),
+        name="open_join",
+    )(parent_blocks)
     joined = pl.pallas_call(
         join_kernel,
         out_shape=jax.ShapeDtypeStruct((2, features, pcol), bf16),
-        in_specs=[VMEM, VMEM, pl.BlockSpec(memory_space=pl.ANY), pl.BlockSpec(memory_space=pl.ANY)],
+        in_specs=[VMEM, VMEM],
         out_specs=VMEM,
         compiler_params=ROOM,
-        cost_estimate=cost(0, 4 * block_bytes),
+        cost_estimate=cost(0, 2 * block_bytes),
         name="join",
-    )(parent_blocks, far, outbox, laid)
+    )(far, half)
     near = exchange(joined, 2)
+    laid = pl.pallas_call(
+        pass_kernel,
+        out_shape=jax.ShapeDtypeStruct(laid.shape, bf16),
+        in_specs=[ANY, ANY],
+        out_specs=ANY,
+        input_output_aliases={0: 0},
+        compiler_params=ROOM,
+        cost_estimate=cost(10**10, 40000 * variables * child_levels * levels),
+        name="behind_join",
+    )(laid, joined)
+    laid, outbox = lax.optimization_barrier((laid, outbox))
+    inbox = lax.all_to_all(outbox, "edge", split_axis=0, concat_axis=0, tiled=True)
     held, rim = pl.pallas_call(
         collect_kernel,
         out_shape=(
@@ -248,7 +276,7 @@
         in_specs=[VMEM, VMEM],
         out_specs=(VMEM, VMEM),
         compiler_params=ROOM,
-        cost_estimate=cost(0, 9 * block_bytes),
+        cost_estimate=cost(10**11, 90000 * block_bytes),
         name="collect",
     )(joined, near)
     rim = across_sides(rim)

time: 50.6 us -> 34.9 us (0.69)
  waiting for transfers between devices: 28.3 us -> 14.5 us
  local copies, waits for them, and re-layouts: 4.24 us -> 1.96 us
    ppermute x4, waiting for transfers between devices: 25.1 us -> 4.07 us  [exchange(): lax.ppermute(array, 'edge', [(i, i ^ distance) for i in range(count)])]
    all_to_all x1, waiting for transfers between devices: 0.01 us -> 6.9 us  [kernel_body(): lax.all_to_all(outbox, 'edge', split_axis=0, concat_axis=0, tiled=True)]
    unnamed x10 -> x4, local copies, waits for them, and re-layouts: 4.24 us -> 1.96 us
    ppermute x4, starting transfers between devices: 3.08 us -> 5.13 us  [exchange(): lax.ppermute(array, 'edge', [(i, i ^ distance) for i in range(count)])]
    all_to_all x1, starting transfers between devices: 6.34 us -> 4.55 us  [kernel_body(): lax.all_to_all(outbox, 'edge', split_axis=0, concat_axis=0, tiled=True)]
  transfers between devices with their start and end apart: 6 -> 6, of which waited for: 4 -> 5; matrix products, arithmetic and copies ran while one was open for 0% -> 0% of each run, Pallas kernels for 1% -> 7%
where the time goes in v4:
time: 34.9 us; the launch traced here: 34.6 us
  waiting for transfers between devices  14.5 us (42%)
  starting transfers between devices  12 us (34%)
  Pallas kernels  6.11 us (18%)
  local copies, waits for them, and re-layouts  1.96 us (6%)
    all_to_all x1, waiting for transfers between devices, kernel_body(): lax.all_to_all(outbox, 'edge', split_axis=0, concat_axis=0, tiled=True)  6.9 us
    ppermute x4, starting transfers between devices, exchange(): lax.ppermute(array, 'edge', [(i, i ^ distance) for i in range(count)])  5.13 us
    all_to_all x1, starting transfers between devices, kernel_body(): lax.all_to_all(outbox, 'edge', split_axis=0, concat_axis=0, tiled=True)  4.55 us
    ppermute x4, waiting for transfers between devices, exchange(): lax.ppermute(array, 'edge', [(i, i ^ distance) for i in range(count)])  4.07 us
    ppermute x1, waiting for transfers between devices, across_sides(): return lax.ppermute(array, AXES, moves)  3.53 us
    pallas_call x1, Pallas kernels, kernel_body(): pl.pallas_call(finish_kernel, out_shape=jax.ShapeDtypeStruct((variables,...  3.52 us
    ppermute x1, starting transfers between devices, across_sides(): return lax.ppermute(array, AXES, moves)  2.32 us
    pallas_call x1, Pallas kernels, kernel_body(): pl.pallas_call(functools.partial(select_kernel, (edge_count, capacity, bl...  2.29 us
  transfers between devices with their start and end apart: 6, of which 5 were waited for; matrix products, arithmetic and copies ran while one was open for 0% of the time, Pallas kernels for 7%

profile of v4, /device:TPU:0, one launch (start us, length us, event | category | flops | bytes accessed | tf_op | source)
XLA Modules:
  0.0 34.6 jit_solution(11871966676733909624)
XLA Ops:
  0.0 4.0 %collective-permute-start = (bf16[1,450,128]{2,1,0:T(8,128)(2,1)}, bf16[1,450,128]{2,1,0:T(8,128)(2,1)S(1)}, u32[]{:S(2)}, u32[]{:S(2)}) collective-permute-start(bf16[1,450,128]{2,1,0:T(8,128)(2,1)} %own_ref.1), channel_id=1, source_target_pairs={{0,4},{1,5},{2,6},{3,7},{4,0},{5,1},{6,2},{7,3},{8,12},{9,13},{10,... | collective-permute-start | bytes 345608 | tf_op jit(solution)/shard_map/ppermute | solution.py:185
  4.0 0.0 copy-start.1
  4.0 0.9 %copy-done.1 = bf16[1,450,128]{2,1,0:T(8,128)(2,1)S(1)} copy-done((bf16[1,450,128]{2,1,0:T(8,128)(2,1)S(1)}, bf16[1,450,128]{2,1,0:T(8,128)(2,1)}, u32[]{:S(2)}) %copy-start.1) | copy-done | bytes 115224
  5.0 0.0 copy-start
  5.0 1.0 %copy-done = bf16[5,400,90]{1,2,0:T(8,128)(2,1)S(1)} copy-done((bf16[5,400,90]{1,2,0:T(8,128)(2,1)S(1)}, bf16[5,400,90]{1,2,0:T(8,128)(2,1)}, u32[]{:S(2)}) %copy-start) | copy-done | bytes 360024
  6.0 0.2 lay_remap.1.laid_ref
  6.3 2.3 %select_weights.1 = bf16[8,264,128]{2,1,0:T(8,128)(2,1)} custom-call(s32[2,4]{1,0:T(2,128)} %bitcast.5, s32[4,128]{1,0:T(4,128)} %bitcast.4, bf16[4,2,128,128]{3,2,1,0:T(8,128)(2,1)} %weight_hbm.1), custom_call_target="tpu_custom_call" | custom-call | flops 276824064 | bytes 540672 | tf_op jit(solution)/shard_map/select_weights/pallas_call | solution.py:214
  8.6 1.4 %collective-permute-done.other_ref = bf16[1,450,128]{2,1,0:T(8,128)(2,1)S(1)} collective-permute-done((bf16[1,450,128]{2,1,0:T(8,128)(2,1)}, bf16[1,450,128]{2,1,0:T(8,128)(2,1)S(1)}, u32[]{:S(2)}, u32[]{:S(2)}) %collective-permute-start) | collective-permute-done | bytes 115232 | tf_op jit(solution)/shard_map/ppermute | solution.py:185
  10.0 0.9 %collective-permute-start.1 = (bf16[2,450,128]{2,1,0:T(8,128)(2,1)S(1)}, bf16[2,450,128]{2,1,0:T(8,128)(2,1)S(1)}, u32[]{:S(2)}, u32[]{:S(2)}) collective-permute-start(bf16[2,450,128]{2,1,0:T(8,128)(2,1)S(1)} %join.1.joined_ref), channel_id=1, source_target_pairs={{0,2},{1,3},{2,0},{3,1},{4,6},{5,7},{6,4},{7,5},{8,10},{9,11},{10,... | collective-permute-start | bytes 691208 | tf_op jit(solution)/shard_map/ppermute | solution.py:185
  10.9 4.6 %all-to-all-start = ((bf16[8,264,128]{2,1,0:T(8,128)(2,1)}), bf16[8,264,128]{2,1,0:T(8,128)(2,1)S(1)}, u32[]{:S(2)}, u32[]{:S(2)}) async-start(bf16[8,264,128]{2,1,0:T(8,128)(2,1)} %select_weights.1), calls=%async_computation | async-start | bytes 1081344 | tf_op jit(solution)/shard_map/all_to_all | solution.py:269
  15.4 1.5 %collective-permute-done.1.near_ref = bf16[2,450,128]{2,1,0:T(8,128)(2,1)S(1)} collective-permute-done((bf16[2,450,128]{2,1,0:T(8,128)(2,1)S(1)}, bf16[2,450,128]{2,1,0:T(8,128)(2,1)S(1)}, u32[]{:S(2)}, u32[]{:S(2)}) %collective-permute-start.1) | collective-permute-done | bytes 230432 | tf_op jit(solution)/shard_map/ppermute | solution.py:185
  16.9 0.1 collective-permute-start.3
  17.0 2.3 %collective-permute-start.2 = (bf16[1,450,128]{2,1,0:T(8,128)(2,1)S(1)}, bf16[1,450,128]{2,1,0:T(8,128)(2,1)S(1)}, u32[]{:S(2)}, u32[]{:S(2)}) collective-permute-start(bf16[1,450,128]{2,1,0:T(8,128)(2,1)S(1)} %get-tuple-element.11), channel_id=1, source_target_pairs={{0,24},{1,9},{2,26},{3,11},{4,28},{5,13},{6,30},{7,15},{8,0},{9,17... | collective-permute-start | bytes 345608 | tf_op jit(solution)/shard_map/ppermute | solution.py:195
  19.3 3.5 %collective-permute-done.2.rim_ref = bf16[1,450,128]{2,1,0:T(8,128)(2,1)S(1)} collective-permute-done((bf16[1,450,128]{2,1,0:T(8,128)(2,1)S(1)}, bf16[1,450,128]{2,1,0:T(8,128)(2,1)S(1)}, u32[]{:S(2)}, u32[]{:S(2)}) %collective-permute-start.2) | collective-permute-done | bytes 115232 | tf_op jit(solution)/shard_map/ppermute | solution.py:195
  22.9 0.1 collective-permute-start.4
  23.0 1.2 %collective-permute-done.4.other_rim_ref = bf16[1,450,128]{2,1,0:T(8,128)(2,1)S(1)} collective-permute-done((bf16[1,450,128]{2,1,0:T(8,128)(2,1)S(1)}, bf16[1,450,128]{2,1,0:T(8,128)(2,1)S(1)}, u32[]{:S(2)}, u32[]{:S(2)}) %collective-permute-start.4) | collective-permute-done | bytes 115232 | tf_op jit(solution)/shard_map/ppermute | solution.py:185
  24.2 0.0 collective-permute-done.3.other_ref
  24.2 6.9 %all-to-all-done.inbox_ref = bf16[8,264,128]{2,1,0:T(8,128)(2,1)S(1)} async-done(((bf16[8,264,128]{2,1,0:T(8,128)(2,1)}), bf16[8,264,128]{2,1,0:T(8,128)(2,1)S(1)}, u32[]{:S(2)}, u32[]{:S(2)}) %all-to-all-start) | async-done | bytes 540704 | tf_op jit(solution)/shard_map/all_to_all | solution.py:269
  31.1 3.5 %finish.1 = bf16[5,400,1024]{2,1,0:T(8,128)(2,1)} custom-call(bf16[8,264,128]{2,1,0:T(8,128)(2,1)S(1)} %all-to-all-done.inbox_ref, bf16[4,450,128]{2,1,0:T(8,128)(2,1)S(1)} %get-tuple-element.10.held_ref, bf16[1,450,128]{2,1,0:T(8,128)(2,1)S(1)} %collective-permute-done.2.rim_ref, bf16[4,450,128]{2,1,0:T(8,128)(2,1)S(1)} %collective-permute-done.3.other_ref, ...), custom_call_target="tpu_custom_call" | custom-call | flops 840499200 | bytes 4096000 | tf_op jit(solution)/shard_map/finish/pallas_call | solution.py:285
  (4 shorter events, 0.1 us)
Async XLA Ops:
  0.0 9.9 %collective-permute-start = (bf16[1,450,128]{2,1,0:T(8,128)(2,1)}, bf16[1,450,128]{2,1,0:T(8,128)(2,1)S(1)}, u32[]{:S(2)}, u32[]{:S(2)}) collective-permute-start(bf16[1,450,128]{2,1,0:T(8,128)(2,1)} %own_ref.1), channel_id=1, source_target_pairs={{0,4},{1,5},{2,6},{3,7},{4,0},{5,1},{6,2},{7,3},{8,12},{9,13},{10,... | collective-permute-start | bytes 345608 | tf_op jit(solution)/shard_map/ppermute | solution.py:185
  4.0 0.9 %copy-start.1 = (bf16[1,450,128]{2,1,0:T(8,128)(2,1)S(1)}, bf16[1,450,128]{2,1,0:T(8,128)(2,1)}, u32[]{:S(2)}) copy-start(bf16[1,450,128]{2,1,0:T(8,128)(2,1)} %own_ref.1) | copy-start | bytes 345604
  5.0 1.0 %copy-start = (bf16[5,400,90]{1,2,0:T(8,128)(2,1)S(1)}, bf16[5,400,90]{1,2,0:T(8,128)(2,1)}, u32[]{:S(2)}) copy-start(bf16[5,400,90]{1,2,0:T(8,128)(2,1)} %param.9) | copy-start | bytes 1080004
  10.0 6.9 %collective-permute-start.1 = (bf16[2,450,128]{2,1,0:T(8,128)(2,1)S(1)}, bf16[2,450,128]{2,1,0:T(8,128)(2,1)S(1)}, u32[]{:S(2)}, u32[]{:S(2)}) collective-permute-start(bf16[2,450,128]{2,1,0:T(8,128)(2,1)S(1)} %join.1.joined_ref), channel_id=1, source_target_pairs={{0,2},{1,3},{2,0},{3,1},{4,6},{5,7},{6,4},{7,5},{8,10},{9,11},{10,... | collective-permute-start | bytes 691208 | tf_op jit(solution)/shard_map/ppermute | solution.py:185
  10.9 20.3 %all-to-all-start = ((bf16[8,264,128]{2,1,0:T(8,128)(2,1)}), bf16[8,264,128]{2,1,0:T(8,128)(2,1)S(1)}, u32[]{:S(2)}, u32[]{:S(2)}) async-start(bf16[8,264,128]{2,1,0:T(8,128)(2,1)} %select_weights.1), calls=%async_computation | async-start | bytes 1081344 | tf_op jit(solution)/shard_map/all_to_all | solution.py:269
  16.9 7.3 %collective-permute-start.3 = (bf16[4,450,128]{2,1,0:T(8,128)(2,1)S(1)}, bf16[4,450,128]{2,1,0:T(8,128)(2,1)S(1)}, u32[]{:S(2)}, u32[]{:S(2)}) collective-permute-start(bf16[4,450,128]{2,1,0:T(8,128)(2,1)S(1)} %get-tuple-element.10.held_ref), channel_id=1, source_target_pairs={{0,1},{1,0},{2,3},{3,2},{4,5},{5,4},{6,7},{7,6},{8,9},{9,8},{10,11... | collective-permute-start | bytes 1382408 | tf_op jit(solution)/shard_map/ppermute | solution.py:185
  17.0 5.9 %collective-permute-start.2 = (bf16[1,450,128]{2,1,0:T(8,128)(2,1)S(1)}, bf16[1,450,128]{2,1,0:T(8,128)(2,1)S(1)}, u32[]{:S(2)}, u32[]{:S(2)}) collective-permute-start(bf16[1,450,128]{2,1,0:T(8,128)(2,1)S(1)} %get-tuple-element.11), channel_id=1, source_target_pairs={{0,24},{1,9},{2,26},{3,11},{4,28},{5,13},{6,30},{7,15},{8,0},{9,17... | collective-permute-start | bytes 345608 | tf_op jit(solution)/shard_map/ppermute | solution.py:195
  22.9 1.3 %collective-permute-start.4 = (bf16[1,450,128]{2,1,0:T(8,128)(2,1)S(1)}, bf16[1,450,128]{2,1,0:T(8,128)(2,1)S(1)}, u32[]{:S(2)}, u32[]{:S(2)}) collective-permute-start(bf16[1,450,128]{2,1,0:T(8,128)(2,1)S(1)} %collective-permute-done.2.rim_ref), channel_id=1, source_target_pairs={{0,1},{1,0},{2,3},{3,2},{4,5},{5,4},{6,7},{7,6},{8,9},{9,8},{10,11... | collective-permute-start | bytes 345608 | tf_op jit(solution)/shard_map/ppermute | solution.py:185

commit v5 on v4

--- a/solution.py
+++ b/solution.py
@@ -99,26 +99,15 @@
         out_ref[v] = turned[:, :WINDOW].astype(jnp.bfloat16)
 
 
-def open_join_kernel(own_ref, out_ref):
-    out_ref[0] = own_ref[0]
-
-
-def join_kernel(other_ref, half_ref, out_ref):
-    out_ref[0] = half_ref[0]
-    out_ref[1] = other_ref[0]
-
-
-def pass_kernel(laid_ref, joined_ref, out_ref):
-    del laid_ref, joined_ref, out_ref
-
-
-def collect_kernel(joined_ref, near_ref, held_ref, rim_ref):
+def pass_kernel(laid_ref, far_ref, out_ref):
+    del laid_ref, far_ref, out_ref
+
+
+def collect_kernel(own_ref, near_ref, far_ref, last_ref, held_ref, rim_ref):
     edge = lax.axis_index("edge")
     place, core = edge // 2, lax.rem(edge, 2)
-    held_ref[0] = joined_ref[0]
-    held_ref[1] = near_ref[0]
-    held_ref[2] = joined_ref[1]
-    held_ref[3] = near_ref[1]
+    for i, ref in enumerate((own_ref, near_ref, far_ref, last_ref)):
+        held_ref[i] = ref[0]
     rim_ref[0] = held_ref[jnp.bitwise_xor(place, 3 * core)]
 
 
@@ -210,6 +199,7 @@
         return pl.CostEstimate(flops=flops, bytes_accessed=bytes_accessed, transcendentals=0)
 
     far = exchange(parent_blocks, 4)
+    near = exchange(parent_blocks, 2)
     height = 2 * pcol + 8
     outbox = pl.pallas_call(
         functools.partial(select_kernel, (edge_count, capacity, block_count)),
@@ -236,25 +226,7 @@
         cost_estimate=cost(0, 4 * variables * child_levels * levels),
         name="lay_remap",
     )(jnp.swapaxes(remap_matrix, 1, 2))
-    half = pl.pallas_call(
-        open_join_kernel,
-        out_shape=jax.ShapeDtypeStruct((2, features, pcol), bf16),
-        in_specs=[VMEM],
-        out_specs=VMEM,
-        compiler_params=ROOM,
-        cost_estimate=cost(0, 4 * block_bytes),
-        name="open_join",
-    )(parent_blocks)
-    joined = pl.pallas_call(
-        join_kernel,
-        out_shape=jax.ShapeDtypeStruct((2, features, pcol), bf16),
-        in_specs=[VMEM, VMEM],
-        out_specs=VMEM,
-        compiler_params=ROOM,
-        cost_estimate=cost(0, 2 * block_bytes),
-        name="join",
-    )(far, half)
-    near = exchange(joined, 2)
+    last = exchange(far, 2)
     laid = pl.pallas_call(
         pass_kernel,
         out_shape=jax.ShapeDtypeStruct(laid.shape, bf16),
@@ -263,8 +235,8 @@
         input_output_aliases={0: 0},
         compiler_params=ROOM,
         cost_estimate=cost(10**10, 40000 * variables * child_levels * levels),
-        name="behind_join",
-    )(laid, joined)
+        name="behind_last",
+    )(laid, far)
     laid, outbox = lax.optimization_barrier((laid, outbox))
     inbox = lax.all_to_all(outbox, "edge", split_axis=0, concat_axis=0, tiled=True)
     held, rim = pl.pallas_call(
@@ -273,12 +245,12 @@
             jax.ShapeDtypeStruct((chips, features, pcol), bf16),
             jax.ShapeDtypeStruct((1, features, pcol), bf16),
         ),
-        in_specs=[VMEM, VMEM],
+        in_specs=[VMEM] * 4,
         out_specs=(VMEM, VMEM),
         compiler_params=ROOM,
         cost_estimate=cost(10**11, 90000 * block_bytes),
         name="collect",
-    )(joined, near)
+    )(parent_blocks, near, far, last)
     rim = across_sides(rim)
     other = exchange(held, 1)
     other_rim = exchange(rim, 1)

time: 34.9 us -> 34.8 us (level)
  starting transfers between devices: 12 us -> 13.9 us
  waiting for transfers between devices: 14.5 us -> 13.5 us
  local copies, waits for them, and re-layouts: 1.96 us -> 1.04 us
    ppermute x4 -> x5, waiting for transfers between devices: 4.07 us -> 2.17 us  [exchange(): lax.ppermute(array, 'edge', [(i, i ^ distance) for i in range(count)])]
    ppermute x4 -> x5, starting transfers between devices: 5.13 us -> 6.9 us  [exchange(): lax.ppermute(array, 'edge', [(i, i ^ distance) for i in range(count)])]
    unnamed x4, local copies, waits for them, and re-layouts: 1.96 us -> 1.04 us
    all_to_all x1, waiting for transfers between devices: 6.9 us -> 7.73 us  [kernel_body(): lax.all_to_all(outbox, 'edge', split_axis=0, concat_axis=0, tiled=True)]
  transfers between devices with their start and end apart: 6 -> 7, of which waited for: 5 -> 4; matrix products, arithmetic and copies ran while one was open for 0% -> 0% of each run, Pallas kernels for 7% -> 7%
where the time goes in v5:
time: 34.8 us; the launch traced here: 34.6 us
  starting transfers between devices  13.9 us (40%)
  waiting for transfers between devices  13.5 us (39%)
  Pallas kernels  6.09 us (18%)
  local copies, waits for them, and re-layouts  1.04 us (3%)
    all_to_all x1, waiting for transfers between devices, kernel_body(): lax.all_to_all(outbox, 'edge', split_axis=0, concat_axis=0, tiled=True)  7.73 us
    ppermute x5, starting transfers between devices, exchange(): lax.ppermute(array, 'edge', [(i, i ^ distance) for i in range(count)])  6.9 us
    all_to_all x1, starting transfers between devices, kernel_body(): lax.all_to_all(outbox, 'edge', split_axis=0, concat_axis=0, tiled=True)  4.55 us
    ppermute x1, waiting for transfers between devices, across_sides(): return lax.ppermute(array, AXES, moves)  3.56 us
    pallas_call x1, Pallas kernels, kernel_body(): pl.pallas_call(finish_kernel, out_shape=jax.ShapeDtypeStruct((variables,...  3.52 us
    ppermute x1, starting transfers between devices, across_sides(): return lax.ppermute(array, AXES, moves)  2.45 us
    pallas_call x1, Pallas kernels, kernel_body(): pl.pallas_call(functools.partial(select_kernel, (edge_count, capacity, bl...  2.29 us
    ppermute x5, waiting for transfers between devices, exchange(): lax.ppermute(array, 'edge', [(i, i ^ distance) for i in range(count)])  2.17 us
  transfers between devices with their start and end apart: 7, of which 4 were waited for; matrix products, arithmetic and copies ran while one was open for 0% of the time, Pallas kernels for 7%

profile of v5, /device:TPU:0, one launch (start us, length us, event | category | flops | bytes accessed | tf_op | source)
XLA Modules:
  0.0 34.6 jit_solution(14201467788170300677)
XLA Ops:
  0.0 4.0 %collective-permute-start = (bf16[1,450,128]{2,1,0:T(8,128)(2,1)}, bf16[1,450,128]{2,1,0:T(8,128)(2,1)S(1)}, u32[]{:S(2)}, u32[]{:S(2)}) collective-permute-start(bf16[1,450,128]{2,1,0:T(8,128)(2,1)} %own_ref.1), channel_id=1, source_target_pairs={{0,4},{1,5},{2,6},{3,7},{4,0},{5,1},{6,2},{7,3},{8,12},{9,13},{10,... | collective-permute-start | bytes 345608 | tf_op jit(solution)/shard_map/ppermute | solution.py:174
  4.0 1.6 %collective-permute-start.1 = (bf16[1,450,128]{2,1,0:T(8,128)(2,1)}, bf16[1,450,128]{2,1,0:T(8,128)(2,1)S(1)}, u32[]{:S(2)}, u32[]{:S(2)}) collective-permute-start(bf16[1,450,128]{2,1,0:T(8,128)(2,1)} %own_ref.1), channel_id=1, source_target_pairs={{0,2},{1,3},{2,0},{3,1},{4,6},{5,7},{6,4},{7,5},{8,10},{9,11},{10,... | collective-permute-start | bytes 345608 | tf_op jit(solution)/shard_map/ppermute | solution.py:174
  5.6 0.0 copy-start
  5.6 1.0 %copy-done = bf16[5,400,90]{1,2,0:T(8,128)(2,1)S(1)} copy-done((bf16[5,400,90]{1,2,0:T(8,128)(2,1)S(1)}, bf16[5,400,90]{1,2,0:T(8,128)(2,1)}, u32[]{:S(2)}) %copy-start) | copy-done | bytes 360024
  6.6 0.2 lay_remap.1.laid_ref
  6.9 2.3 %select_weights.1 = bf16[8,264,128]{2,1,0:T(8,128)(2,1)} custom-call(s32[2,4]{1,0:T(2,128)} %bitcast.5, s32[4,128]{1,0:T(4,128)} %bitcast.4, bf16[4,2,128,128]{3,2,1,0:T(8,128)(2,1)} %weight_hbm.1), custom_call_target="tpu_custom_call" | custom-call | flops 276824064 | bytes 540672 | tf_op jit(solution)/shard_map/select_weights/pallas_call | solution.py:204
  9.2 0.0 copy-start.1
  9.2 0.8 %collective-permute-done.far_ref = bf16[1,450,128]{2,1,0:T(8,128)(2,1)S(1)} collective-permute-done((bf16[1,450,128]{2,1,0:T(8,128)(2,1)}, bf16[1,450,128]{2,1,0:T(8,128)(2,1)S(1)}, u32[]{:S(2)}, u32[]{:S(2)}) %collective-permute-start) | collective-permute-done | bytes 115232 | tf_op jit(solution)/shard_map/ppermute | solution.py:174
  10.0 0.7 %collective-permute-start.2 = (bf16[1,450,128]{2,1,0:T(8,128)(2,1)S(1)}, bf16[1,450,128]{2,1,0:T(8,128)(2,1)S(1)}, u32[]{:S(2)}, u32[]{:S(2)}) collective-permute-start(bf16[1,450,128]{2,1,0:T(8,128)(2,1)S(1)} %collective-permute-done.far_ref), channel_id=1, source_target_pairs={{0,2},{1,3},{2,0},{3,1},{4,6},{5,7},{6,4},{7,5},{8,10},{9,11},{10,... | collective-permute-start | bytes 345608 | tf_op jit(solution)/shard_map/ppermute | solution.py:174
  10.8 4.6 %all-to-all-start = ((bf16[8,264,128]{2,1,0:T(8,128)(2,1)}), bf16[8,264,128]{2,1,0:T(8,128)(2,1)S(1)}, u32[]{:S(2)}, u32[]{:S(2)}) async-start(bf16[8,264,128]{2,1,0:T(8,128)(2,1)} %select_weights.1), calls=%async_computation | async-start | bytes 1081344 | tf_op jit(solution)/shard_map/all_to_all | solution.py:241
  15.3 0.0 collective-permute-done.1.near_ref
  15.3 0.0 collective-permute-done.2.last_ref
  15.3 0.0 copy-done.1
  15.4 0.6 %collective-permute-start.4 = (bf16[4,450,128]{2,1,0:T(8,128)(2,1)S(1)}, bf16[4,450,128]{2,1,0:T(8,128)(2,1)S(1)}, u32[]{:S(2)}, u32[]{:S(2)}) collective-permute-start(bf16[4,450,128]{2,1,0:T(8,128)(2,1)S(1)} %get-tuple-element.10.held_ref), channel_id=1, source_target_pairs={{0,1},{1,0},{2,3},{3,2},{4,5},{5,4},{6,7},{7,6},{8,9},{9,8},{10,11... | collective-permute-start | bytes 1382408 | tf_op jit(solution)/shard_map/ppermute | solution.py:174
  16.0 2.4 %collective-permute-start.3 = (bf16[1,450,128]{2,1,0:T(8,128)(2,1)S(1)}, bf16[1,450,128]{2,1,0:T(8,128)(2,1)S(1)}, u32[]{:S(2)}, u32[]{:S(2)}) collective-permute-start(bf16[1,450,128]{2,1,0:T(8,128)(2,1)S(1)} %get-tuple-element.11), channel_id=1, source_target_pairs={{0,24},{1,9},{2,26},{3,11},{4,28},{5,13},{6,30},{7,15},{8,0},{9,17... | collective-permute-start | bytes 345608 | tf_op jit(solution)/shard_map/ppermute | solution.py:184
  18.4 3.6 %collective-permute-done.3.rim_ref = bf16[1,450,128]{2,1,0:T(8,128)(2,1)S(1)} collective-permute-done((bf16[1,450,128]{2,1,0:T(8,128)(2,1)S(1)}, bf16[1,450,128]{2,1,0:T(8,128)(2,1)S(1)}, u32[]{:S(2)}, u32[]{:S(2)}) %collective-permute-start.3) | collective-permute-done | bytes 115232 | tf_op jit(solution)/shard_map/ppermute | solution.py:184
  22.0 0.0 collective-permute-start.5
  22.0 1.3 %collective-permute-done.5.other_rim_ref = bf16[1,450,128]{2,1,0:T(8,128)(2,1)S(1)} collective-permute-done((bf16[1,450,128]{2,1,0:T(8,128)(2,1)S(1)}, bf16[1,450,128]{2,1,0:T(8,128)(2,1)S(1)}, u32[]{:S(2)}, u32[]{:S(2)}) %collective-permute-start.5) | collective-permute-done | bytes 115232 | tf_op jit(solution)/shard_map/ppermute | solution.py:174
  23.3 0.0 collective-permute-done.4.other_ref
  23.3 7.7 %all-to-all-done.inbox_ref = bf16[8,264,128]{2,1,0:T(8,128)(2,1)S(1)} async-done(((bf16[8,264,128]{2,1,0:T(8,128)(2,1)}), bf16[8,264,128]{2,1,0:T(8,128)(2,1)S(1)}, u32[]{:S(2)}, u32[]{:S(2)}) %all-to-all-start) | async-done | bytes 540704 | tf_op jit(solution)/shard_map/all_to_all | solution.py:241
  31.0 3.5 %finish.1 = bf16[5,400,1024]{2,1,0:T(8,128)(2,1)} custom-call(bf16[8,264,128]{2,1,0:T(8,128)(2,1)S(1)} %all-to-all-done.inbox_ref, bf16[4,450,128]{2,1,0:T(8,128)(2,1)S(1)} %get-tuple-element.10.held_ref, bf16[1,450,128]{2,1,0:T(8,128)(2,1)S(1)} %collective-permute-done.3.rim_ref, bf16[4,450,128]{2,1,0:T(8,128)(2,1)S(1)} %collective-permute-done.4.other_ref, ...), custom_call_target="tpu_custom_call" | custom-call | flops 840499200 | bytes 4096000 | tf_op jit(solution)/shard_map/finish/pallas_call | solution.py:257
  (2 shorter events, 0.0 us)
Async XLA Ops:
  0.0 10.0 %collective-permute-start = (bf16[1,450,128]{2,1,0:T(8,128)(2,1)}, bf16[1,450,128]{2,1,0:T(8,128)(2,1)S(1)}, u32[]{:S(2)}, u32[]{:S(2)}) collective-permute-start(bf16[1,450,128]{2,1,0:T(8,128)(2,1)} %own_ref.1), channel_id=1, source_target_pairs={{0,4},{1,5},{2,6},{3,7},{4,0},{5,1},{6,2},{7,3},{8,12},{9,13},{10,... | collective-permute-start | bytes 345608 | tf_op jit(solution)/shard_map/ppermute | solution.py:174
  4.0 11.3 %collective-permute-start.1 = (bf16[1,450,128]{2,1,0:T(8,128)(2,1)}, bf16[1,450,128]{2,1,0:T(8,128)(2,1)S(1)}, u32[]{:S(2)}, u32[]{:S(2)}) collective-permute-start(bf16[1,450,128]{2,1,0:T(8,128)(2,1)} %own_ref.1), channel_id=1, source_target_pairs={{0,2},{1,3},{2,0},{3,1},{4,6},{5,7},{6,4},{7,5},{8,10},{9,11},{10,... | collective-permute-start | bytes 345608 | tf_op jit(solution)/shard_map/ppermute | solution.py:174
  5.6 1.0 %copy-start = (bf16[5,400,90]{1,2,0:T(8,128)(2,1)S(1)}, bf16[5,400,90]{1,2,0:T(8,128)(2,1)}, u32[]{:S(2)}) copy-start(bf16[5,400,90]{1,2,0:T(8,128)(2,1)} %param.9) | copy-start | bytes 1080004
  9.2 6.2 %copy-start.1 = (bf16[1,450,128]{2,1,0:T(8,128)(2,1)S(1)}, bf16[1,450,128]{2,1,0:T(8,128)(2,1)}, u32[]{:S(2)}) copy-start(bf16[1,450,128]{2,1,0:T(8,128)(2,1)} %own_ref.1) | copy-start | bytes 345604
  10.0 5.3 %collective-permute-start.2 = (bf16[1,450,128]{2,1,0:T(8,128)(2,1)S(1)}, bf16[1,450,128]{2,1,0:T(8,128)(2,1)S(1)}, u32[]{:S(2)}, u32[]{:S(2)}) collective-permute-start(bf16[1,450,128]{2,1,0:T(8,128)(2,1)S(1)} %collective-permute-done.far_ref), channel_id=1, source_target_pairs={{0,2},{1,3},{2,0},{3,1},{4,6},{5,7},{6,4},{7,5},{8,10},{9,11},{10,... | collective-permute-start | bytes 345608 | tf_op jit(solution)/shard_map/ppermute | solution.py:174
  10.8 20.3 %all-to-all-start = ((bf16[8,264,128]{2,1,0:T(8,128)(2,1)}), bf16[8,264,128]{2,1,0:T(8,128)(2,1)S(1)}, u32[]{:S(2)}, u32[]{:S(2)}) async-start(bf16[8,264,128]{2,1,0:T(8,128)(2,1)} %select_weights.1), calls=%async_computation | async-start | bytes 1081344 | tf_op jit(solution)/shard_map/all_to_all | solution.py:241
  15.4 7.9 %collective-permute-start.4 = (bf16[4,450,128]{2,1,0:T(8,128)(2,1)S(1)}, bf16[4,450,128]{2,1,0:T(8,128)(2,1)S(1)}, u32[]{:S(2)}, u32[]{:S(2)}) collective-permute-start(bf16[4,450,128]{2,1,0:T(8,128)(2,1)S(1)} %get-tuple-element.10.held_ref), channel_id=1, source_target_pairs={{0,1},{1,0},{2,3},{3,2},{4,5},{5,4},{6,7},{7,6},{8,9},{9,8},{10,11... | collective-permute-start | bytes 1382408 | tf_op jit(solution)/shard_map/ppermute | solution.py:174
  16.0 6.0 %collective-permute-start.3 = (bf16[1,450,128]{2,1,0:T(8,128)(2,1)S(1)}, bf16[1,450,128]{2,1,0:T(8,128)(2,1)S(1)}, u32[]{:S(2)}, u32[]{:S(2)}) collective-permute-start(bf16[1,450,128]{2,1,0:T(8,128)(2,1)S(1)} %get-tuple-element.11), channel_id=1, source_target_pairs={{0,24},{1,9},{2,26},{3,11},{4,28},{5,13},{6,30},{7,15},{8,0},{9,17... | collective-permute-start | bytes 345608 | tf_op jit(solution)/shard_map/ppermute | solution.py:184
  22.0 1.3 %collective-permute-start.5 = (bf16[1,450,128]{2,1,0:T(8,128)(2,1)S(1)}, bf16[1,450,128]{2,1,0:T(8,128)(2,1)S(1)}, u32[]{:S(2)}, u32[]{:S(2)}) collective-permute-start(bf16[1,450,128]{2,1,0:T(8,128)(2,1)S(1)} %collective-permute-done.3.rim_ref), channel_id=1, source_target_pairs={{0,1},{1,0},{2,3},{3,2},{4,5},{5,4},{6,7},{7,6},{8,9},{9,8},{10,11... | collective-permute-start | bytes 345608 | tf_op jit(solution)/shard_map/ppermute | solution.py:174

commit v6 on v5

--- a/solution.py
+++ b/solution.py
@@ -99,8 +99,8 @@
         out_ref[v] = turned[:, :WINDOW].astype(jnp.bfloat16)
 
 
-def pass_kernel(laid_ref, far_ref, out_ref):
-    del laid_ref, far_ref, out_ref
+def pass_kernel(in_ref, out_ref):
+    del in_ref, out_ref
 
 
 def collect_kernel(own_ref, near_ref, far_ref, last_ref, held_ref, rim_ref):
@@ -112,59 +112,60 @@
 
 
 def finish_kernel(
-    inbox_ref, held_ref, rim_ref, other_ref, other_rim_ref, remap_ref, out_hbm, coarse, result, sems
+    inbox_ref, held_ref, rim_ref, other_ref, other_rim_ref, remap_ref, out_hbm, parents, coarse, result, sems
 ):
     edge = lax.axis_index("edge")
     place, core = edge // 2, lax.rem(edge, 2)
-    variables, child_levels, _ = remap_ref.shape
-    features = held_ref.shape[1]
+    variables = remap_ref.shape[0]
+    features, pcol = held_ref.shape[1:]
     levels = features // variables
-    pcol = held_ref.shape[2]
-    capacity = inbox_ref.shape[2]
-    chips = inbox_ref.shape[0] // 2
-
-    def block(chip, parity):
-        inside = jnp.logical_and(chip >= 0, chip < chips)
-        where = jnp.bitwise_and(jnp.bitwise_xor(chip, place), chips - 1)
-        mine = jnp.where(inside, held_ref[where], rim_ref[0])
-        theirs = jnp.where(inside, other_ref[where], other_rim_ref[0])
-        return jnp.where(core == parity, mine, theirs)
-
-    copies = []
-    for step in range(chips):
-        chip = jnp.bitwise_xor(place, step)
-        parents = jnp.concatenate(
-            [block(chip - 1, 1), block(chip, 0), block(chip, 1), block(chip + 1, 0)], axis=1
-        )
+    owners, _, capacity = inbox_ref.shape
+    chips = owners // 2
+
+    for i in range(owners + 2):
+        chip, parity = divmod(i - 1, 2)
+        if 0 <= chip < chips:
+            where = jnp.bitwise_xor(place, chip)
+            mine, theirs = held_ref[where], other_ref[where]
+        else:
+            mine, theirs = rim_ref[0], other_rim_ref[0]
+        parents[0:features, i * pcol : (i + 1) * pcol] = jnp.where(core == parity, mine, theirs)
+
+    def kept(condition):
+        return condition.astype(jnp.float32).astype(jnp.bfloat16)
+
+    width = 2 * capacity
+    for chip in range(chips):
         columns = []
         for parity in range(2):
-            sent = inbox_ref.at[2 * chip + parity]
-            low, high = sent[0:pcol, :], sent[pcol : 2 * pcol, :]
-            left_out = jnp.broadcast_to(sent[2 * pcol : 2 * pcol + 1, :].astype(jnp.float32), (pcol, capacity))
-            zero = jnp.zeros_like(low)
+            source = 2 * chip + parity
+            low, high = inbox_ref[source, 0:pcol, :], inbox_ref[source, pcol : 2 * pcol, :]
+            left_out = inbox_ref[source, 2 * pcol : 2 * pcol + 1, :].astype(jnp.float32)
             parts = [
-                jnp.where(left_out > 0.5, low, zero),
-                jnp.where(left_out < 0.5, low, jnp.where(left_out > 1.5, high, zero)),
-                jnp.where(left_out < 1.5, high, zero),
+                low * kept(left_out > 0.5),
+                low * kept(left_out < 0.5) + high * kept(left_out > 1.5),
+                high * kept(left_out < 1.5),
             ]
-            parts.insert(3 if parity == 0 else 0, zero)
+            parts.insert(3 if parity == 0 else 0, jnp.zeros_like(low))
             columns.append(jnp.concatenate(parts, axis=0))
-        coarse[step, 0:features, :] = jnp.dot(
-            parents, jnp.concatenate(columns, axis=1), preferred_element_type=jnp.float32
+        coarse[0:features, chip * width : (chip + 1) * width] = jnp.dot(
+            parents[0:features, chip * 2 * pcol : (chip * 2 + 4) * pcol],
+            jnp.concatenate(columns, axis=1),
+            preferred_element_type=jnp.float32,
         ).astype(jnp.bfloat16)
-        rest = coarse.shape[1] - features
-        coarse[step, features:, :] = jnp.zeros((rest, 2 * capacity), jnp.bfloat16)
-        for v in range(variables):
-            first, _ = window_of(v, levels)
-            result[step, v] = jnp.dot(
-                remap_ref[v],
-                coarse[step, first : first + WINDOW, :],
-                preferred_element_type=jnp.float32,
+    rest = coarse.shape[0] - features
+    coarse[features:, :] = jnp.zeros((rest, owners * capacity), jnp.bfloat16)
+    copies = []
+    for v in range(variables):
+        first, _ = window_of(v, levels)
+        for chip in range(chips):
+            lanes = slice(chip * width, (chip + 1) * width)
+            result[v, :, lanes] = jnp.dot(
+                remap_ref[v], coarse[first : first + WINDOW, lanes], preferred_element_type=jnp.float32
             ).astype(jnp.bfloat16)
-            slots = pl.ds(pl.multiple_of(chip * 2 * capacity, 2 * capacity), 2 * capacity)
-            copy = pltpu.make_async_copy(result.at[step, v], out_hbm.at[v, :, slots], sems.at[step, v])
-            copy.start()
-            copies.append(copy)
+        copy = pltpu.make_async_copy(result.at[v], out_hbm.at[v], sems.at[v])
+        copy.start()
+        copies.append(copy)
     for copy in copies:
         copy.wait()
 
@@ -226,18 +227,18 @@
         cost_estimate=cost(0, 4 * variables * child_levels * levels),
         name="lay_remap",
     )(jnp.swapaxes(remap_matrix, 1, 2))
-    last = exchange(far, 2)
-    laid = pl.pallas_call(
+    last = exchange(parent_blocks, 6)
+    near = pl.pallas_call(
         pass_kernel,
-        out_shape=jax.ShapeDtypeStruct(laid.shape, bf16),
-        in_specs=[ANY, ANY],
+        out_shape=jax.ShapeDtypeStruct(near.shape, bf16),
+        in_specs=[ANY],
         out_specs=ANY,
         input_output_aliases={0: 0},
         compiler_params=ROOM,
-        cost_estimate=cost(10**10, 40000 * variables * child_levels * levels),
-        name="behind_last",
-    )(laid, far)
-    laid, outbox = lax.optimization_barrier((laid, outbox))
+        cost_estimate=cost(10**10, 10**9),
+        name="behind_near",
+    )(near)
+    near, outbox = lax.optimization_barrier((near, outbox))
     inbox = lax.all_to_all(outbox, "edge", split_axis=0, concat_axis=0, tiled=True)
     held, rim = pl.pallas_call(
         collect_kernel,
@@ -260,9 +261,10 @@
         in_specs=[VMEM] * 6,
         out_specs=HBM,
         scratch_shapes=[
-            pltpu.VMEM((chips, 464, 2 * capacity), bf16),
-            pltpu.VMEM((chips, variables, child_levels, 2 * capacity), bf16),
-            pltpu.SemaphoreType.DMA((chips, variables)),
+            pltpu.VMEM((464, (edge_count + 2) * pcol), bf16),
+            pltpu.VMEM((464, slots), bf16),
+            pltpu.VMEM((variables, child_levels, slots), bf16),
+            pltpu.SemaphoreType.DMA((variables,)),
         ],
         compiler_params=ROOM,
         cost_estimate=cost(

time: 34.8 us -> 32.1 us (0.922)
  local copies, waits for them, and re-layouts: 1.04 us -> 0.01 us
  waiting for transfers between devices: 13.5 us -> 12.8 us
  Pallas kernels: 6.09 us -> 5.59 us
  starting transfers between devices: 13.9 us -> 13.4 us
    ppermute x5, starting transfers between devices: 6.9 us -> 5.71 us  [exchange(): lax.ppermute(array, 'edge', [(i, i ^ distance) for i in range(count)])]
    all_to_all x1, waiting for transfers between devices: 7.73 us -> 6.57 us  [kernel_body(): lax.all_to_all(outbox, 'edge', split_axis=0, concat_axis=0, tiled=True)]
    unnamed x4, local copies, waits for them, and re-layouts: 1.04 us -> 0.01 us
    ppermute x5, waiting for transfers between devices: 2.17 us -> 2.98 us  [exchange(): lax.ppermute(array, 'edge', [(i, i ^ distance) for i in range(count)])]
    all_to_all x1, starting transfers between devices: 4.55 us -> 5.23 us  [kernel_body(): lax.all_to_all(outbox, 'edge', split_axis=0, concat_axis=0, tiled=True)]
    pallas_call x1, Pallas kernels: 3.52 us -> 3.02 us  [kernel_body(): pl.pallas_call(finish_kernel, out_shape=jax.ShapeDtypeStruct((variables,...]
  transfers between devices with their start and end apart: 7 -> 7, of which waited for: 4 -> 4; matrix products, arithmetic and copies ran while one was open for 0% -> 0% of each run, Pallas kernels for 7% -> 8%
where the time goes in v6:
time: 32.1 us; the launch traced here: 31.9 us
  starting transfers between devices  13.4 us (42%)
  waiting for transfers between devices  12.8 us (40%)
  Pallas kernels  5.59 us (17%)
    all_to_all x1, waiting for transfers between devices, kernel_body(): lax.all_to_all(outbox, 'edge', split_axis=0, concat_axis=0, tiled=True)  6.57 us
    ppermute x5, starting transfers between devices, exchange(): lax.ppermute(array, 'edge', [(i, i ^ distance) for i in range(count)])  5.71 us
    all_to_all x1, starting transfers between devices, kernel_body(): lax.all_to_all(outbox, 'edge', split_axis=0, concat_axis=0, tiled=True)  5.23 us
    ppermute x1, waiting for transfers between devices, across_sides(): return lax.ppermute(array, AXES, moves)  3.26 us
    pallas_call x1, Pallas kernels, kernel_body(): pl.pallas_call(finish_kernel, out_shape=jax.ShapeDtypeStruct((variables,...  3.02 us
    ppermute x5, waiting for transfers between devices, exchange(): lax.ppermute(array, 'edge', [(i, i ^ distance) for i in range(count)])  2.98 us
    ppermute x1, starting transfers between devices, across_sides(): return lax.ppermute(array, AXES, moves)  2.5 us
    pallas_call x1, Pallas kernels, kernel_body(): pl.pallas_call(functools.partial(select_kernel, (edge_count, capacity, bl...  2.3 us
  transfers between devices with their start and end apart: 7, of which 4 were waited for; matrix products, arithmetic and copies ran while one was open for 0% of the time, Pallas kernels for 8%

profile of v6, /device:TPU:0, one launch (start us, length us, event | category | flops | bytes accessed | tf_op | source)
XLA Modules:
  0.0 31.9 jit_solution(3159115312077729467)
XLA Ops:
  0.0 3.0 %collective-permute-start = (bf16[1,450,128]{2,1,0:T(8,128)(2,1)}, bf16[1,450,128]{2,1,0:T(8,128)(2,1)S(1)}, u32[]{:S(2)}, u32[]{:S(2)}) collective-permute-start(bf16[1,450,128]{2,1,0:T(8,128)(2,1)} %own_ref.1), channel_id=1, source_target_pairs={{0,2},{1,3},{2,0},{3,1},{4,6},{5,7},{6,4},{7,5},{8,10},{9,11},{10,... | collective-permute-start | bytes 345608 | tf_op jit(solution)/shard_map/ppermute | solution.py:175
  3.0 2.6 %collective-permute-start.1 = (bf16[1,450,128]{2,1,0:T(8,128)(2,1)}, bf16[1,450,128]{2,1,0:T(8,128)(2,1)S(1)}, u32[]{:S(2)}, u32[]{:S(2)}) collective-permute-start(bf16[1,450,128]{2,1,0:T(8,128)(2,1)} %own_ref.1), channel_id=1, source_target_pairs={{0,4},{1,5},{2,6},{3,7},{4,0},{5,1},{6,2},{7,3},{8,12},{9,13},{10,... | collective-permute-start | bytes 345608 | tf_op jit(solution)/shard_map/ppermute | solution.py:175
  5.6 0.0 collective-permute-start.2
  5.6 2.3 %select_weights.1 = bf16[8,264,128]{2,1,0:T(8,128)(2,1)} custom-call(s32[2,4]{1,0:T(2,128)} %bitcast.5, s32[4,128]{1,0:T(4,128)} %bitcast.4, bf16[4,2,128,128]{3,2,1,0:T(8,128)(2,1)} %weight_hbm.1), custom_call_target="tpu_custom_call" | custom-call | flops 276824064 | bytes 540672 | tf_op jit(solution)/shard_map/select_weights/pallas_call | solution.py:205
  7.9 0.0 copy-start.1
  7.9 0.0 collective-permute-done.in_ref
  8.0 5.2 %all-to-all-start = ((bf16[8,264,128]{2,1,0:T(8,128)(2,1)}), bf16[8,264,128]{2,1,0:T(8,128)(2,1)S(1)}, u32[]{:S(2)}, u32[]{:S(2)}) async-start(bf16[8,264,128]{2,1,0:T(8,128)(2,1)} %select_weights.1), calls=%async_computation | async-start | bytes 1081344 | tf_op jit(solution)/shard_map/all_to_all | solution.py:242
  13.2 0.0 copy-start
  13.2 1.9 %collective-permute-done.1.far_ref = bf16[1,450,128]{2,1,0:T(8,128)(2,1)S(1)} collective-permute-done((bf16[1,450,128]{2,1,0:T(8,128)(2,1)}, bf16[1,450,128]{2,1,0:T(8,128)(2,1)S(1)}, u32[]{:S(2)}, u32[]{:S(2)}) %collective-permute-start.1) | collective-permute-done | bytes 115232 | tf_op jit(solution)/shard_map/ppermute | solution.py:175
  15.1 0.0 collective-permute-done.2.last_ref
  15.1 0.0 copy-done.1
  15.2 0.1 collective-permute-start.4
  15.2 2.5 %collective-permute-start.3 = (bf16[1,450,128]{2,1,0:T(8,128)(2,1)S(1)}, bf16[1,450,128]{2,1,0:T(8,128)(2,1)S(1)}, u32[]{:S(2)}, u32[]{:S(2)}) collective-permute-start(bf16[1,450,128]{2,1,0:T(8,128)(2,1)S(1)} %get-tuple-element.12), channel_id=1, source_target_pairs={{0,24},{1,9},{2,26},{3,11},{4,28},{5,13},{6,30},{7,15},{8,0},{9,17... | collective-permute-start | bytes 345608 | tf_op jit(solution)/shard_map/ppermute | solution.py:185
  17.7 3.3 %collective-permute-done.3.rim_ref = bf16[1,450,128]{2,1,0:T(8,128)(2,1)S(1)} collective-permute-done((bf16[1,450,128]{2,1,0:T(8,128)(2,1)S(1)}, bf16[1,450,128]{2,1,0:T(8,128)(2,1)S(1)}, u32[]{:S(2)}, u32[]{:S(2)}) %collective-permute-start.3) | collective-permute-done | bytes 115232 | tf_op jit(solution)/shard_map/ppermute | solution.py:185
  21.0 0.0 collective-permute-start.5
  21.0 0.0 copy-done
  21.0 0.2 lay_remap.1.remap_ref
  21.3 1.1 %collective-permute-done.5.other_rim_ref = bf16[1,450,128]{2,1,0:T(8,128)(2,1)S(1)} collective-permute-done((bf16[1,450,128]{2,1,0:T(8,128)(2,1)S(1)}, bf16[1,450,128]{2,1,0:T(8,128)(2,1)S(1)}, u32[]{:S(2)}, u32[]{:S(2)}) %collective-permute-start.5) | collective-permute-done | bytes 115232 | tf_op jit(solution)/shard_map/ppermute | solution.py:175
  22.3 0.0 collective-permute-done.4.other_ref
  22.3 6.6 %all-to-all-done.inbox_ref = bf16[8,264,128]{2,1,0:T(8,128)(2,1)S(1)} async-done(((bf16[8,264,128]{2,1,0:T(8,128)(2,1)}), bf16[8,264,128]{2,1,0:T(8,128)(2,1)S(1)}, u32[]{:S(2)}, u32[]{:S(2)}) %all-to-all-start) | async-done | bytes 540704 | tf_op jit(solution)/shard_map/all_to_all | solution.py:242
  28.9 3.0 %finish.1 = bf16[5,400,1024]{2,1,0:T(8,128)(2,1)} custom-call(bf16[8,264,128]{2,1,0:T(8,128)(2,1)S(1)} %all-to-all-done.inbox_ref, bf16[4,450,128]{2,1,0:T(8,128)(2,1)S(1)} %get-tuple-element.11.held_ref, bf16[1,450,128]{2,1,0:T(8,128)(2,1)S(1)} %collective-permute-done.3.rim_ref, bf16[4,450,128]{2,1,0:T(8,128)(2,1)S(1)} %collective-permute-done.4.other_ref, ...), custom_call_target="tpu_custom_call" | custom-call | flops 840499200 | bytes 4096000 | tf_op jit(solution)/shard_map/finish/pallas_call | solution.py:258
  (2 shorter events, 0.0 us)
Async XLA Ops:
  0.0 7.9 %collective-permute-start = (bf16[1,450,128]{2,1,0:T(8,128)(2,1)}, bf16[1,450,128]{2,1,0:T(8,128)(2,1)S(1)}, u32[]{:S(2)}, u32[]{:S(2)}) collective-permute-start(bf16[1,450,128]{2,1,0:T(8,128)(2,1)} %own_ref.1), channel_id=1, source_target_pairs={{0,2},{1,3},{2,0},{3,1},{4,6},{5,7},{6,4},{7,5},{8,10},{9,11},{10,... | collective-permute-start | bytes 345608 | tf_op jit(solution)/shard_map/ppermute | solution.py:175
  3.0 12.1 %collective-permute-start.1 = (bf16[1,450,128]{2,1,0:T(8,128)(2,1)}, bf16[1,450,128]{2,1,0:T(8,128)(2,1)S(1)}, u32[]{:S(2)}, u32[]{:S(2)}) collective-permute-start(bf16[1,450,128]{2,1,0:T(8,128)(2,1)} %own_ref.1), channel_id=1, source_target_pairs={{0,4},{1,5},{2,6},{3,7},{4,0},{5,1},{6,2},{7,3},{8,12},{9,13},{10,... | collective-permute-start | bytes 345608 | tf_op jit(solution)/shard_map/ppermute | solution.py:175
  5.6 9.5 %collective-permute-start.2 = (bf16[1,450,128]{2,1,0:T(8,128)(2,1)}, bf16[1,450,128]{2,1,0:T(8,128)(2,1)S(1)}, u32[]{:S(2)}, u32[]{:S(2)}) collective-permute-start(bf16[1,450,128]{2,1,0:T(8,128)(2,1)} %own_ref.1), channel_id=1, source_target_pairs={{0,6},{1,7},{2,4},{3,5},{4,2},{5,3},{6,0},{7,1},{8,14},{9,15},{10,... | collective-permute-start | bytes 345608 | tf_op jit(solution)/shard_map/ppermute | solution.py:175
  7.9 7.2 %copy-start.1 = (bf16[1,450,128]{2,1,0:T(8,128)(2,1)S(1)}, bf16[1,450,128]{2,1,0:T(8,128)(2,1)}, u32[]{:S(2)}) copy-start(bf16[1,450,128]{2,1,0:T(8,128)(2,1)} %own_ref.1) | copy-start | bytes 345604
  8.0 20.9 %all-to-all-start = ((bf16[8,264,128]{2,1,0:T(8,128)(2,1)}), bf16[8,264,128]{2,1,0:T(8,128)(2,1)S(1)}, u32[]{:S(2)}, u32[]{:S(2)}) async-start(bf16[8,264,128]{2,1,0:T(8,128)(2,1)} %select_weights.1), calls=%async_computation | async-start | bytes 1081344 | tf_op jit(solution)/shard_map/all_to_all | solution.py:242
  13.2 7.8 %copy-start = (bf16[5,400,90]{1,2,0:T(8,128)(2,1)S(1)}, bf16[5,400,90]{1,2,0:T(8,128)(2,1)}, u32[]{:S(2)}) copy-start(bf16[5,400,90]{1,2,0:T(8,128)(2,1)} %param.9) | copy-start | bytes 1080004
  15.2 7.2 %collective-permute-start.4 = (bf16[4,450,128]{2,1,0:T(8,128)(2,1)S(1)}, bf16[4,450,128]{2,1,0:T(8,128)(2,1)S(1)}, u32[]{:S(2)}, u32[]{:S(2)}) collective-permute-start(bf16[4,450,128]{2,1,0:T(8,128)(2,1)S(1)} %get-tuple-element.11.held_ref), channel_id=1, source_target_pairs={{0,1},{1,0},{2,3},{3,2},{4,5},{5,4},{6,7},{7,6},{8,9},{9,8},{10,11... | collective-permute-start | bytes 1382408 | tf_op jit(solution)/shard_map/ppermute | solution.py:175
  15.2 5.8 %collective-permute-start.3 = (bf16[1,450,128]{2,1,0:T(8,128)(2,1)S(1)}, bf16[1,450,128]{2,1,0:T(8,128)(2,1)S(1)}, u32[]{:S(2)}, u32[]{:S(2)}) collective-permute-start(bf16[1,450,128]{2,1,0:T(8,128)(2,1)S(1)} %get-tuple-element.12), channel_id=1, source_target_pairs={{0,24},{1,9},{2,26},{3,11},{4,28},{5,13},{6,30},{7,15},{8,0},{9,17... | collective-permute-start | bytes 345608 | tf_op jit(solution)/shard_map/ppermute | solution.py:185
  21.0 1.3 %collective-permute-start.5 = (bf16[1,450,128]{2,1,0:T(8,128)(2,1)S(1)}, bf16[1,450,128]{2,1,0:T(8,128)(2,1)S(1)}, u32[]{:S(2)}, u32[]{:S(2)}) collective-permute-start(bf16[1,450,128]{2,1,0:T(8,128)(2,1)S(1)} %collective-permute-done.3.rim_ref), channel_id=1, source_target_pairs={{0,1},{1,0},{2,3},{3,2},{4,5},{5,4},{6,7},{7,6},{8,9},{9,8},{10,11... | collective-permute-start | bytes 345608 | tf_op jit(solution)/shard_map/ppermute | solution.py:175

commit v7 on v6

--- a/solution.py
+++ b/solution.py
@@ -47,7 +47,9 @@
     return first, v * levels - first
 
 
-def select_kernel(sizes, source_hbm, dest_hbm, weight_hbm, out_ref, source, dest, weight, spread, sems):
+def select_kernel(
+    sizes, source_hbm, dest_hbm, weight_hbm, out_ref, kept_ref, given_ref, source, dest, weight, spread, sems
+):
     owner_count, capacity, block_count = sizes
     tiles, _, pcol, rows = weight.shape
     copies = [
@@ -85,6 +87,9 @@
         ).astype(jnp.bfloat16)
         for i in range(pair):
             out_ref[c * pair + i] = picked[:height, i * capacity : (i + 1) * capacity]
+    edge = lax.axis_index("edge")
+    kept_ref[...] = out_ref[edge]
+    given_ref[...] = out_ref[jnp.bitwise_xor(edge, 1)]
 
 
 def lay_remap_kernel(remap_ref, out_ref):
@@ -111,16 +116,30 @@
     rim_ref[0] = held_ref[jnp.bitwise_xor(place, 3 * core)]
 
 
-def finish_kernel(
-    inbox_ref, held_ref, rim_ref, other_ref, other_rim_ref, remap_ref, out_hbm, parents, coarse, result, sems
+def spread_weights(rows, parity, pcol):
+    def kept(condition):
+        return condition.astype(jnp.float32).astype(jnp.bfloat16)
+
+    low, high = rows[0:pcol, :], rows[pcol : 2 * pcol, :]
+    left_out = rows[2 * pcol : 2 * pcol + 1, :].astype(jnp.float32)
+    parts = [
+        low * kept(left_out > 0.5),
+        low * kept(left_out < 0.5) + high * kept(left_out > 1.5),
+        high * kept(left_out < 1.5),
+    ]
+    parts.insert(3 if parity == 0 else 0, jnp.zeros_like(low))
+    return jnp.concatenate(parts, axis=0)
+
+
+def begin_kernel(
+    own_ref, crossed_ref, held_ref, rim_ref, other_ref, other_rim_ref, remap_ref, parents, begun, coarse
 ):
     edge = lax.axis_index("edge")
     place, core = edge // 2, lax.rem(edge, 2)
     variables = remap_ref.shape[0]
-    features, pcol = held_ref.shape[1:]
+    chips, features, pcol = held_ref.shape
     levels = features // variables
-    owners, _, capacity = inbox_ref.shape
-    chips = owners // 2
+    owners = 2 * chips
 
     for i in range(owners + 2):
         chip, parity = divmod(i - 1, 2)
@@ -130,42 +149,65 @@
         else:
             mine, theirs = rim_ref[0], other_rim_ref[0]
         parents[0:features, i * pcol : (i + 1) * pcol] = jnp.where(core == parity, mine, theirs)
-
-    def kept(condition):
-        return condition.astype(jnp.float32).astype(jnp.bfloat16)
-
+    columns = [
+        spread_weights(jnp.where(core == parity, own_ref[...], crossed_ref[...]), parity, pcol)
+        for parity in range(2)
+    ]
+    blocks = pl.ds(pl.multiple_of(place * 2 * pcol, 2 * pcol), 4 * pcol)
+    coarse[0:features, :] = jnp.dot(
+        parents[0:features, blocks],
+        jnp.concatenate(columns, axis=1),
+        preferred_element_type=jnp.float32,
+    ).astype(jnp.bfloat16)
+    coarse[features:, :] = jnp.zeros((coarse.shape[0] - features, coarse.shape[1]), jnp.bfloat16)
+    for v in range(variables):
+        first, _ = window_of(v, levels)
+        begun[v] = jnp.dot(
+            remap_ref[v], coarse[first : first + WINDOW, :], preferred_element_type=jnp.float32
+        ).astype(jnp.bfloat16)
+
+
+def finish_kernel(levels, inbox_ref, parents_ref, begun_ref, remap_ref, out_hbm, coarse, result, sems):
+    place = lax.axis_index("edge") // 2
+    variables, child_levels, _ = remap_ref.shape
+    owners, _, capacity = inbox_ref.shape
+    pcol = parents_ref.shape[1] // (owners + 2)
+    features = levels * variables
     width = 2 * capacity
-    for chip in range(chips):
-        columns = []
-        for parity in range(2):
-            source = 2 * chip + parity
-            low, high = inbox_ref[source, 0:pcol, :], inbox_ref[source, pcol : 2 * pcol, :]
-            left_out = inbox_ref[source, 2 * pcol : 2 * pcol + 1, :].astype(jnp.float32)
-            parts = [
-                low * kept(left_out > 0.5),
-                low * kept(left_out < 0.5) + high * kept(left_out > 1.5),
-                high * kept(left_out < 1.5),
-            ]
-            parts.insert(3 if parity == 0 else 0, jnp.zeros_like(low))
-            columns.append(jnp.concatenate(parts, axis=0))
-        coarse[0:features, chip * width : (chip + 1) * width] = jnp.dot(
-            parents[0:features, chip * 2 * pcol : (chip * 2 + 4) * pcol],
+    away = range(1, owners // 2)
+    for distance in away:
+        chip = jnp.bitwise_xor(place, distance)
+        columns = [
+            spread_weights(inbox_ref[2 * chip + parity], parity, pcol) for parity in range(2)
+        ]
+        blocks = pl.ds(pl.multiple_of(chip * 2 * pcol, 2 * pcol), 4 * pcol)
+        coarse[0:features, (distance - 1) * width : distance * width] = jnp.dot(
+            parents_ref[0:features, blocks],
             jnp.concatenate(columns, axis=1),
             preferred_element_type=jnp.float32,
         ).astype(jnp.bfloat16)
-    rest = coarse.shape[0] - features
-    coarse[features:, :] = jnp.zeros((rest, owners * capacity), jnp.bfloat16)
+    coarse[features:, :] = jnp.zeros((coarse.shape[0] - features, coarse.shape[1]), jnp.bfloat16)
     copies = []
     for v in range(variables):
         first, _ = window_of(v, levels)
-        for chip in range(chips):
-            lanes = slice(chip * width, (chip + 1) * width)
-            result[v, :, lanes] = jnp.dot(
-                remap_ref[v], coarse[first : first + WINDOW, lanes], preferred_element_type=jnp.float32
-            ).astype(jnp.bfloat16)
-        copy = pltpu.make_async_copy(result.at[v], out_hbm.at[v], sems.at[v])
-        copy.start()
-        copies.append(copy)
+        cuts = [0, child_levels] if v < variables - 1 else [0, child_levels // 32 * 16, child_levels]
+        for low, high in zip(cuts[:-1], cuts[1:]):
+            for distance in range(owners // 2):
+                chip = jnp.bitwise_xor(place, distance)
+                lanes = pl.ds(pl.multiple_of(chip * width, width), width)
+                if distance == 0:
+                    result[v, low:high, lanes] = begun_ref[v, low:high, :]
+                else:
+                    result[v, low:high, lanes] = jnp.dot(
+                        remap_ref[v, low:high, :],
+                        coarse[first : first + WINDOW, (distance - 1) * width : distance * width],
+                        preferred_element_type=jnp.float32,
+                    ).astype(jnp.bfloat16)
+            copy = pltpu.make_async_copy(
+                result.at[v, low:high], out_hbm.at[v, low:high], sems.at[len(copies)]
+            )
+            copy.start()
+            copies.append(copy)
     for copy in copies:
         copy.wait()
 
@@ -202,11 +244,15 @@
     far = exchange(parent_blocks, 4)
     near = exchange(parent_blocks, 2)
     height = 2 * pcol + 8
-    outbox = pl.pallas_call(
+    outbox, on_chip, given = pl.pallas_call(
         functools.partial(select_kernel, (edge_count, capacity, block_count)),
-        out_shape=jax.ShapeDtypeStruct((edge_count, height, capacity), bf16),
+        out_shape=(
+            jax.ShapeDtypeStruct((edge_count, height, capacity), bf16),
+            jax.ShapeDtypeStruct((height, capacity), bf16),
+            jax.ShapeDtypeStruct((height, capacity), bf16),
+        ),
         in_specs=[HBM, HBM, HBM],
-        out_specs=VMEM,
+        out_specs=(VMEM, VMEM, VMEM),
         scratch_shapes=[
             pltpu.SMEM((2, tiles), jnp.int32),
             pltpu.VMEM((tiles, tile_rows), jnp.int32),
@@ -252,27 +298,46 @@
         cost_estimate=cost(10**11, 90000 * block_bytes),
         name="collect",
     )(parent_blocks, near, far, last)
+    held, given = lax.optimization_barrier((held, given))
     rim = across_sides(rim)
     other = exchange(held, 1)
     other_rim = exchange(rim, 1)
+    crossed = exchange(given, 1)
+    padded = -(-features // 16) * 16
+    parents, begun = pl.pallas_call(
+        begin_kernel,
+        out_shape=(
+            jax.ShapeDtypeStruct((padded, (edge_count + 2) * pcol), bf16),
+            jax.ShapeDtypeStruct((variables, child_levels, 2 * capacity), bf16),
+        ),
+        in_specs=[VMEM] * 7,
+        out_specs=(VMEM, VMEM),
+        scratch_shapes=[pltpu.VMEM((padded, 2 * capacity), bf16)],
+        compiler_params=ROOM,
+        cost_estimate=cost(
+            4 * capacity * (4 * pcol * features + variables * child_levels * levels),
+            2 * variables * child_levels * slots,
+        ),
+        name="begin",
+    )(on_chip, crossed, held, rim, other, other_rim, laid)
+    away = slots - 2 * capacity
     return pl.pallas_call(
-        finish_kernel,
+        functools.partial(finish_kernel, levels),
         out_shape=jax.ShapeDtypeStruct((variables, child_levels, slots), bf16),
-        in_specs=[VMEM] * 6,
+        in_specs=[VMEM] * 4,
         out_specs=HBM,
         scratch_shapes=[
-            pltpu.VMEM((464, (edge_count + 2) * pcol), bf16),
-            pltpu.VMEM((464, slots), bf16),
+            pltpu.VMEM((padded, away), bf16),
             pltpu.VMEM((variables, child_levels, slots), bf16),
-            pltpu.SemaphoreType.DMA((variables,)),
+            pltpu.SemaphoreType.DMA((variables + 1,)),
         ],
         compiler_params=ROOM,
         cost_estimate=cost(
-            2 * slots * (4 * pcol * features + variables * child_levels * levels),
+            2 * away * (4 * pcol * features + variables * child_levels * levels),
             2 * variables * child_levels * slots,
         ),
         name="finish",
-    )(inbox, held, rim, other, other_rim, laid)
+    )(inbox, parents, begun, laid)
 
 
 def plain_body(parent_blocks, interp_weight, tile_source, destination, remap_matrix):

time: 32.1 us -> 32 us (level)
  waiting for transfers between devices: 12.8 us -> 11.2 us
  Pallas kernels: 5.59 us -> 6.5 us
  starting transfers between devices: 13.4 us -> 13.9 us
    all_to_all x1, waiting for transfers between devices: 6.57 us -> 5.4 us  [kernel_body(): lax.all_to_all(outbox, 'edge', split_axis=0, concat_axis=0, tiled=True)]
    pallas_call x1 -> x2, Pallas kernels: 3.02 us -> 3.91 us  [the longest x1 2.83 us: kernel_body(): pl.pallas_call(functools.partial(finish_kernel, levels), out_shape=jax.Sh...]
    ppermute x5 -> x6, starting transfers between devices: 5.71 us -> 6.2 us  [exchange(): lax.ppermute(array, 'edge', [(i, i ^ distance) for i in range(count)])]
    ppermute x5 -> x6, waiting for transfers between devices: 2.98 us -> 2.54 us  [exchange(): lax.ppermute(array, 'edge', [(i, i ^ distance) for i in range(count)])]
  transfers between devices with their start and end apart: 7 -> 8, of which waited for: 4 -> 4; matrix products, arithmetic and copies ran while one was open for 0% -> 0% of each run, Pallas kernels for 8% -> 12%
where the time goes in v7:
time: 32 us; the launch traced here: 31.7 us
  starting transfers between devices  13.9 us (43%)
  waiting for transfers between devices  11.2 us (35%)
  Pallas kernels  6.5 us (20%)
    ppermute x6, starting transfers between devices, exchange(): lax.ppermute(array, 'edge', [(i, i ^ distance) for i in range(count)])  6.2 us
    all_to_all x1, waiting for transfers between devices, kernel_body(): lax.all_to_all(outbox, 'edge', split_axis=0, concat_axis=0, tiled=True)  5.4 us
    all_to_all x1, starting transfers between devices, kernel_body(): lax.all_to_all(outbox, 'edge', split_axis=0, concat_axis=0, tiled=True)  5.23 us
    ppermute x1, waiting for transfers between devices, across_sides(): return lax.ppermute(array, AXES, moves)  3.26 us
    pallas_call x1, Pallas kernels, kernel_body(): pl.pallas_call(functools.partial(finish_kernel, levels), out_shape=jax.Sh...  2.83 us
    ppermute x6, waiting for transfers between devices, exchange(): lax.ppermute(array, 'edge', [(i, i ^ distance) for i in range(count)])  2.54 us
    ppermute x1, starting transfers between devices, across_sides(): return lax.ppermute(array, AXES, moves)  2.5 us
    pallas_call x1, Pallas kernels, kernel_body(): pl.pallas_call(functools.partial(select_kernel, (edge_count, capacity, bl...  2.31 us
  transfers between devices with their start and end apart: 8, of which 4 were waited for; matrix products, arithmetic and copies ran while one was open for 0% of the time, Pallas kernels for 12%

profile of v7, /device:TPU:0, one launch (start us, length us, event | category | flops | bytes accessed | tf_op | source)
XLA Modules:
  0.0 31.7 jit_solution(8380602408541824568)
XLA Ops:
  0.0 3.0 %collective-permute-start = (bf16[1,450,128]{2,1,0:T(8,128)(2,1)}, bf16[1,450,128]{2,1,0:T(8,128)(2,1)S(1)}, u32[]{:S(2)}, u32[]{:S(2)}) collective-permute-start(bf16[1,450,128]{2,1,0:T(8,128)(2,1)} %own_ref.1), channel_id=1, source_target_pairs={{0,2},{1,3},{2,0},{3,1},{4,6},{5,7},{6,4},{7,5},{8,10},{9,11},{10,... | collective-permute-start | bytes 345608 | tf_op jit(solution)/shard_map/ppermute | solution.py:217
  3.0 2.6 %collective-permute-start.1 = (bf16[1,450,128]{2,1,0:T(8,128)(2,1)}, bf16[1,450,128]{2,1,0:T(8,128)(2,1)S(1)}, u32[]{:S(2)}, u32[]{:S(2)}) collective-permute-start(bf16[1,450,128]{2,1,0:T(8,128)(2,1)} %own_ref.1), channel_id=1, source_target_pairs={{0,4},{1,5},{2,6},{3,7},{4,0},{5,1},{6,2},{7,3},{8,12},{9,13},{10,... | collective-permute-start | bytes 345608 | tf_op jit(solution)/shard_map/ppermute | solution.py:217
  5.6 0.0 collective-permute-start.2
  5.6 2.3 %select_weights.1 = (bf16[8,264,128]{2,1,0:T(8,128)(2,1)}, bf16[264,128]{1,0:T(8,128)(2,1)}, bf16[264,128]{1,0:T(8,128)(2,1)}) custom-call(s32[2,4]{1,0:T(2,128)} %bitcast.5, s32[4,128]{1,0:T(4,128)} %bitcast.4, bf16[4,2,128,128]{3,2,1,0:T(8,128)(2,1)} %weight_hbm.1), custom_call_target="tpu_custom_call" | custom-call | flops 276824064 | bytes 540672 | tf_op jit(solution)/shard_map/select_weights/pallas_call | solution.py:247
  7.9 0.0 copy-start.2
  7.9 0.0 collective-permute-done.in_ref
  8.0 5.2 %all-to-all-start = ((bf16[8,264,128]{2,1,0:T(8,128)(2,1)}), bf16[8,264,128]{2,1,0:T(8,128)(2,1)S(1)}, u32[]{:S(2)}, u32[]{:S(2)}) async-start(bf16[8,264,128]{2,1,0:T(8,128)(2,1)} %get-tuple-element.17), calls=%async_computation | async-start | bytes 1081344 | tf_op jit(solution)/shard_map/all_to_all | solution.py:288
  13.2 0.0 copy-start.3
  13.2 0.0 copy-start
  13.2 0.0 copy-start.1
  13.2 1.9 %collective-permute-done.1.far_ref = bf16[1,450,128]{2,1,0:T(8,128)(2,1)S(1)} collective-permute-done((bf16[1,450,128]{2,1,0:T(8,128)(2,1)}, bf16[1,450,128]{2,1,0:T(8,128)(2,1)S(1)}, u32[]{:S(2)}, u32[]{:S(2)}) %collective-permute-start.1) | collective-permute-done | bytes 115232 | tf_op jit(solution)/shard_map/ppermute | solution.py:217
  15.1 0.0 collective-permute-done.2.last_ref
  15.1 0.0 copy-done.2
  15.2 0.1 collective-permute-start.5
  15.2 2.5 %collective-permute-start.4 = (bf16[1,450,128]{2,1,0:T(8,128)(2,1)S(1)}, bf16[1,450,128]{2,1,0:T(8,128)(2,1)S(1)}, u32[]{:S(2)}, u32[]{:S(2)}) collective-permute-start(bf16[1,450,128]{2,1,0:T(8,128)(2,1)S(1)} %get-tuple-element.24), channel_id=1, source_target_pairs={{0,24},{1,9},{2,26},{3,11},{4,28},{5,13},{6,30},{7,15},{8,0},{9,17... | collective-permute-start | bytes 345608 | tf_op jit(solution)/shard_map/ppermute | solution.py:227
  17.7 3.3 %collective-permute-done.4.rim_ref = bf16[1,450,128]{2,1,0:T(8,128)(2,1)S(1)} collective-permute-done((bf16[1,450,128]{2,1,0:T(8,128)(2,1)S(1)}, bf16[1,450,128]{2,1,0:T(8,128)(2,1)S(1)}, u32[]{:S(2)}, u32[]{:S(2)}) %collective-permute-start.4) | collective-permute-done | bytes 115232 | tf_op jit(solution)/shard_map/ppermute | solution.py:227
  21.0 0.0 collective-permute-start.6
  21.0 0.0 copy-done.3
  21.0 0.5 %collective-permute-start.3 = (bf16[264,128]{1,0:T(8,128)(2,1)S(1)}, bf16[264,128]{1,0:T(8,128)(2,1)S(1)}, u32[]{:S(2)}, u32[]{:S(2)}) collective-permute-start(bf16[264,128]{1,0:T(8,128)(2,1)S(1)} %copy-done.3), channel_id=1, source_target_pairs={{0,1},{1,0},{2,3},{3,2},{4,5},{5,4},{6,7},{7,6},{8,9},{9,8},{10,11... | collective-permute-start | bytes 202760 | tf_op jit(solution)/shard_map/ppermute | solution.py:217
  21.5 0.0 copy-done
  21.5 0.2 lay_remap.1.remap_ref
  21.8 0.7 %collective-permute-done.3.crossed_ref = bf16[264,128]{1,0:T(8,128)(2,1)S(1)} collective-permute-done((bf16[264,128]{1,0:T(8,128)(2,1)S(1)}, bf16[264,128]{1,0:T(8,128)(2,1)S(1)}, u32[]{:S(2)}, u32[]{:S(2)}) %collective-permute-start.3) | collective-permute-done | bytes 67616 | tf_op jit(solution)/shard_map/ppermute | solution.py:217
  22.4 0.0 collective-permute-done.6.other_rim_ref
  22.4 0.0 collective-permute-done.5.other_ref
  22.4 0.0 copy-done.1
  22.4 1.1 %begin.1 = (bf16[464,1280]{1,0:T(8,128)(2,1)S(1)}, bf16[5,400,256]{2,1,0:T(8,128)(2,1)S(1)}) custom-call(bf16[264,128]{1,0:T(8,128)(2,1)S(1)} %copy-done.1, bf16[264,128]{1,0:T(8,128)(2,1)S(1)} %collective-permute-done.3.crossed_ref, bf16[4,450,128]{2,1,0:T(8,128)(2,1)S(1)} %get-tuple-element.23.held_ref, ...), custom_call_target="tpu_custom_call" | custom-call | flops 210124800 | bytes 4096000 | tf_op jit(solution)/shard_map/begin/pallas_call | solution.py:307
  23.5 5.4 %all-to-all-done.inbox_ref = bf16[8,264,128]{2,1,0:T(8,128)(2,1)S(1)} async-done(((bf16[8,264,128]{2,1,0:T(8,128)(2,1)}), bf16[8,264,128]{2,1,0:T(8,128)(2,1)S(1)}, u32[]{:S(2)}, u32[]{:S(2)}) %all-to-all-start) | async-done | bytes 540704 | tf_op jit(solution)/shard_map/all_to_all | solution.py:288
  28.9 2.8 %finish.1 = bf16[5,400,1024]{2,1,0:T(8,128)(2,1)} custom-call(bf16[8,264,128]{2,1,0:T(8,128)(2,1)S(1)} %all-to-all-done.inbox_ref, bf16[464,1280]{1,0:T(8,128)(2,1)S(1)} %get-tuple-element.25.parents_ref, bf16[5,400,256]{2,1,0:T(8,128)(2,1)S(1)} %get-tuple-element.26.begun_ref, bf16[5,400,112]{2,1,0:T(8,128)(2,1)S(1)} %lay_remap.1.remap_ref), custom_call_target="tpu_custom_call" | custom-call | flops 630374400 | bytes 4096000 | tf_op jit(solution)/shard_map/finish/pallas_call | solution.py:324
  (2 shorter events, 0.0 us)
Async XLA Ops:
  0.0 8.0 %collective-permute-start = (bf16[1,450,128]{2,1,0:T(8,128)(2,1)}, bf16[1,450,128]{2,1,0:T(8,128)(2,1)S(1)}, u32[]{:S(2)}, u32[]{:S(2)}) collective-permute-start(bf16[1,450,128]{2,1,0:T(8,128)(2,1)} %own_ref.1), channel_id=1, source_target_pairs={{0,2},{1,3},{2,0},{3,1},{4,6},{5,7},{6,4},{7,5},{8,10},{9,11},{10,... | collective-permute-start | bytes 345608 | tf_op jit(solution)/shard_map/ppermute | solution.py:217
  3.0 12.1 %collective-permute-start.1 = (bf16[1,450,128]{2,1,0:T(8,128)(2,1)}, bf16[1,450,128]{2,1,0:T(8,128)(2,1)S(1)}, u32[]{:S(2)}, u32[]{:S(2)}) collective-permute-start(bf16[1,450,128]{2,1,0:T(8,128)(2,1)} %own_ref.1), channel_id=1, source_target_pairs={{0,4},{1,5},{2,6},{3,7},{4,0},{5,1},{6,2},{7,3},{8,12},{9,13},{10,... | collective-permute-start | bytes 345608 | tf_op jit(solution)/shard_map/ppermute | solution.py:217
  5.6 9.5 %collective-permute-start.2 = (bf16[1,450,128]{2,1,0:T(8,128)(2,1)}, bf16[1,450,128]{2,1,0:T(8,128)(2,1)S(1)}, u32[]{:S(2)}, u32[]{:S(2)}) collective-permute-start(bf16[1,450,128]{2,1,0:T(8,128)(2,1)} %own_ref.1), channel_id=1, source_target_pairs={{0,6},{1,7},{2,4},{3,5},{4,2},{5,3},{6,0},{7,1},{8,14},{9,15},{10,... | collective-permute-start | bytes 345608 | tf_op jit(solution)/shard_map/ppermute | solution.py:217
  7.9 7.2 %copy-start.2 = (bf16[1,450,128]{2,1,0:T(8,128)(2,1)S(1)}, bf16[1,450,128]{2,1,0:T(8,128)(2,1)}, u32[]{:S(2)}) copy-start(bf16[1,450,128]{2,1,0:T(8,128)(2,1)} %own_ref.1) | copy-start | bytes 345604
  8.0 20.9 %all-to-all-start = ((bf16[8,264,128]{2,1,0:T(8,128)(2,1)}), bf16[8,264,128]{2,1,0:T(8,128)(2,1)S(1)}, u32[]{:S(2)}, u32[]{:S(2)}) async-start(bf16[8,264,128]{2,1,0:T(8,128)(2,1)} %get-tuple-element.17), calls=%async_computation | async-start | bytes 1081344 | tf_op jit(solution)/shard_map/all_to_all | solution.py:288
  13.2 7.8 %copy-start.3 = (bf16[264,128]{1,0:T(8,128)(2,1)S(1)}, bf16[264,128]{1,0:T(8,128)(2,1)}, u32[]{:S(2)}) copy-start(bf16[264,128]{1,0:T(8,128)(2,1)} %get-tuple-element.22) | copy-start | bytes 202756
  13.2 8.3 %copy-start = (bf16[5,400,90]{1,2,0:T(8,128)(2,1)S(1)}, bf16[5,400,90]{1,2,0:T(8,128)(2,1)}, u32[]{:S(2)}) copy-start(bf16[5,400,90]{1,2,0:T(8,128)(2,1)} %param.9) | copy-start | bytes 1080004
  13.2 9.2 %copy-start.1 = (bf16[264,128]{1,0:T(8,128)(2,1)S(1)}, bf16[264,128]{1,0:T(8,128)(2,1)}, u32[]{:S(2)}) copy-start(bf16[264,128]{1,0:T(8,128)(2,1)} %get-tuple-element.18.own_ref) | copy-start | bytes 202756
  15.2 7.3 %collective-permute-start.5 = (bf16[4,450,128]{2,1,0:T(8,128)(2,1)S(1)}, bf16[4,450,128]{2,1,0:T(8,128)(2,1)S(1)}, u32[]{:S(2)}, u32[]{:S(2)}) collective-permute-start(bf16[4,450,128]{2,1,0:T(8,128)(2,1)S(1)} %get-tuple-element.23.held_ref), channel_id=1, source_target_pairs={{0,1},{1,0},{2,3},{3,2},{4,5},{5,4},{6,7},{7,6},{8,9},{9,8},{10,11... | collective-permute-start | bytes 1382408 | tf_op jit(solution)/shard_map/ppermute | solution.py:217
  15.2 5.8 %collective-permute-start.4 = (bf16[1,450,128]{2,1,0:T(8,128)(2,1)S(1)}, bf16[1,450,128]{2,1,0:T(8,128)(2,1)S(1)}, u32[]{:S(2)}, u32[]{:S(2)}) collective-permute-start(bf16[1,450,128]{2,1,0:T(8,128)(2,1)S(1)} %get-tuple-element.24), channel_id=1, source_target_pairs={{0,24},{1,9},{2,26},{3,11},{4,28},{5,13},{6,30},{7,15},{8,0},{9,17... | collective-permute-start | bytes 345608 | tf_op jit(solution)/shard_map/ppermute | solution.py:227
  21.0 1.4 %collective-permute-start.6 = (bf16[1,450,128]{2,1,0:T(8,128)(2,1)S(1)}, bf16[1,450,128]{2,1,0:T(8,128)(2,1)S(1)}, u32[]{:S(2)}, u32[]{:S(2)}) collective-permute-start(bf16[1,450,128]{2,1,0:T(8,128)(2,1)S(1)} %collective-permute-done.4.rim_ref), channel_id=1, source_target_pairs={{0,1},{1,0},{2,3},{3,2},{4,5},{5,4},{6,7},{7,6},{8,9},{9,8},{10,11... | collective-permute-start | bytes 345608 | tf_op jit(solution)/shard_map/ppermute | solution.py:217
  21.0 1.4 %collective-permute-start.3 = (bf16[264,128]{1,0:T(8,128)(2,1)S(1)}, bf16[264,128]{1,0:T(8,128)(2,1)S(1)}, u32[]{:S(2)}, u32[]{:S(2)}) collective-permute-start(bf16[264,128]{1,0:T(8,128)(2,1)S(1)} %copy-done.3), channel_id=1, source_target_pairs={{0,1},{1,0},{2,3},{3,2},{4,5},{5,4},{6,7},{7,6},{8,9},{9,8},{10,11... | collective-permute-start | bytes 202760 | tf_op jit(solution)/shard_map/ppermute | solution.py:217

commit v8 on v7

--- a/solution.py
+++ b/solution.py
@@ -132,7 +132,18 @@
 
 
 def begin_kernel(
-    own_ref, crossed_ref, held_ref, rim_ref, other_ref, other_rim_ref, remap_ref, parents, begun, coarse
+    own_ref,
+    crossed_ref,
+    held_ref,
+    rim_ref,
+    other_ref,
+    other_rim_ref,
+    remap_ref,
+    parents,
+    out_hbm,
+    coarse,
+    result,
+    sems,
 ):
     edge = lax.axis_index("edge")
     place, core = edge // 2, lax.rem(edge, 2)
@@ -160,16 +171,24 @@
         preferred_element_type=jnp.float32,
     ).astype(jnp.bfloat16)
     coarse[features:, :] = jnp.zeros((coarse.shape[0] - features, coarse.shape[1]), jnp.bfloat16)
+    slots = pl.ds(pl.multiple_of(place * coarse.shape[1], coarse.shape[1]), coarse.shape[1])
+    copies = []
     for v in range(variables):
         first, _ = window_of(v, levels)
-        begun[v] = jnp.dot(
+        result[v] = jnp.dot(
             remap_ref[v], coarse[first : first + WINDOW, :], preferred_element_type=jnp.float32
         ).astype(jnp.bfloat16)
-
-
-def finish_kernel(levels, inbox_ref, parents_ref, begun_ref, remap_ref, out_hbm, coarse, result, sems):
+        copy = pltpu.make_async_copy(result.at[v], out_hbm.at[v, :, slots], sems.at[v])
+        copy.start()
+        copies.append(copy)
+    for copy in copies:
+        copy.wait()
+
+
+def finish_kernel(levels, inbox_ref, parents_ref, remap_ref, begun_hbm, out_hbm, coarse, result, sems):
+    del begun_hbm
     place = lax.axis_index("edge") // 2
-    variables, child_levels, _ = remap_ref.shape
+    variables = remap_ref.shape[0]
     owners, _, capacity = inbox_ref.shape
     pcol = parents_ref.shape[1] // (owners + 2)
     features = levels * variables
@@ -190,21 +209,17 @@
     copies = []
     for v in range(variables):
         first, _ = window_of(v, levels)
-        cuts = [0, child_levels] if v < variables - 1 else [0, child_levels // 32 * 16, child_levels]
-        for low, high in zip(cuts[:-1], cuts[1:]):
-            for distance in range(owners // 2):
-                chip = jnp.bitwise_xor(place, distance)
-                lanes = pl.ds(pl.multiple_of(chip * width, width), width)
-                if distance == 0:
-                    result[v, low:high, lanes] = begun_ref[v, low:high, :]
-                else:
-                    result[v, low:high, lanes] = jnp.dot(
-                        remap_ref[v, low:high, :],
-                        coarse[first : first + WINDOW, (distance - 1) * width : distance * width],
-                        preferred_element_type=jnp.float32,
-                    ).astype(jnp.bfloat16)
+        for distance in away:
+            result[distance - 1, v] = jnp.dot(
+                remap_ref[v],
+                coarse[first : first + WINDOW, (distance - 1) * width : distance * width],
+                preferred_element_type=jnp.float32,
+            ).astype(jnp.bfloat16)
+        for distance in away:
+            chip = jnp.bitwise_xor(place, distance)
+            slots = pl.ds(pl.multiple_of(chip * width, width), width)
             copy = pltpu.make_async_copy(
-                result.at[v, low:high], out_hbm.at[v, low:high], sems.at[len(copies)]
+                result.at[distance - 1, v], out_hbm.at[v, :, slots], sems.at[distance - 1, v]
             )
             copy.start()
             copies.append(copy)
@@ -308,11 +323,15 @@
         begin_kernel,
         out_shape=(
             jax.ShapeDtypeStruct((padded, (edge_count + 2) * pcol), bf16),
-            jax.ShapeDtypeStruct((variables, child_levels, 2 * capacity), bf16),
+            jax.ShapeDtypeStruct((variables, child_levels, slots), bf16),
         ),
         in_specs=[VMEM] * 7,
-        out_specs=(VMEM, VMEM),
-        scratch_shapes=[pltpu.VMEM((padded, 2 * capacity), bf16)],
+        out_specs=(VMEM, HBM),
+        scratch_shapes=[
+            pltpu.VMEM((padded, 2 * capacity), bf16),
+            pltpu.VMEM((variables, child_levels, 2 * capacity), bf16),
+            pltpu.SemaphoreType.DMA((variables,)),
+        ],
         compiler_params=ROOM,
         cost_estimate=cost(
             4 * capacity * (4 * pcol * features + variables * child_levels * levels),
@@ -324,20 +343,21 @@
     return pl.pallas_call(
         functools.partial(finish_kernel, levels),
         out_shape=jax.ShapeDtypeStruct((variables, child_levels, slots), bf16),
-        in_specs=[VMEM] * 4,
+        in_specs=[VMEM] * 3 + [HBM],
         out_specs=HBM,
         scratch_shapes=[
             pltpu.VMEM((padded, away), bf16),
-            pltpu.VMEM((variables, child_levels, slots), bf16),
-            pltpu.SemaphoreType.DMA((variables + 1,)),
+            pltpu.VMEM((chips - 1, variables, child_levels, 2 * capacity), bf16),
+            pltpu.SemaphoreType.DMA((chips - 1, variables)),
         ],
+        input_output_aliases={3: 0},
         compiler_params=ROOM,
         cost_estimate=cost(
             2 * away * (4 * pcol * features + variables * child_levels * levels),
             2 * variables * child_levels * slots,
         ),
         name="finish",
-    )(inbox, parents, begun, laid)
+    )(inbox, parents, laid, begun)
 
 
 def plain_body(parent_blocks, interp_weight, tile_source, destination, remap_matrix):

time: 32 us -> 31.7 us (level)
  waiting for transfers between devices: 11.2 us -> 10.4 us
  Pallas kernels: 6.5 us -> 7.05 us
    pallas_call x1, Pallas kernels: 1.08 us -> 1.84 us  [kernel_body(): pl.pallas_call(begin_kernel, out_shape=(jax.ShapeDtypeStruct((padded, (ed...]
    all_to_all x1, waiting for transfers between devices: 5.4 us -> 4.65 us  [kernel_body(): lax.all_to_all(outbox, 'edge', split_axis=0, concat_axis=0, tiled=True)]
  transfers between devices with their start and end apart: 8 -> 8, of which waited for: 4 -> 4; matrix products, arithmetic and copies ran while one was open for 0% -> 0% of each run, Pallas kernels for 12% -> 14%
where the time goes in v8:
time: 31.7 us; the launch traced here: 31.5 us
  starting transfers between devices  13.9 us (44%)
  waiting for transfers between devices  10.4 us (33%)
  Pallas kernels  7.05 us (22%)
    ppermute x6, starting transfers between devices, exchange(): lax.ppermute(array, 'edge', [(i, i ^ distance) for i in range(count)])  6.2 us
    all_to_all x1, starting transfers between devices, kernel_body(): lax.all_to_all(outbox, 'edge', split_axis=0, concat_axis=0, tiled=True)  5.23 us
    all_to_all x1, waiting for transfers between devices, kernel_body(): lax.all_to_all(outbox, 'edge', split_axis=0, concat_axis=0, tiled=True)  4.65 us
    ppermute x1, waiting for transfers between devices, across_sides(): return lax.ppermute(array, AXES, moves)  3.26 us
    pallas_call x1, Pallas kernels, kernel_body(): pl.pallas_call(functools.partial(finish_kernel, levels), out_shape=jax.Sh...  2.6 us
    ppermute x6, waiting for transfers between devices, exchange(): lax.ppermute(array, 'edge', [(i, i ^ distance) for i in range(count)])  2.52 us
    ppermute x1, starting transfers between devices, across_sides(): return lax.ppermute(array, AXES, moves)  2.5 us
    pallas_call x1, Pallas kernels, kernel_body(): pl.pallas_call(functools.partial(select_kernel, (edge_count, capacity, bl...  2.33 us
  transfers between devices with their start and end apart: 8, of which 4 were waited for; matrix products, arithmetic and copies ran while one was open for 0% of the time, Pallas kernels for 14%

profile of v8, /device:TPU:0, one launch (start us, length us, event | category | flops | bytes accessed | tf_op | source)
XLA Modules:
  0.0 31.5 jit_solution(4449341438580920266)
XLA Ops:
  0.0 3.0 %collective-permute-start = (bf16[1,450,128]{2,1,0:T(8,128)(2,1)}, bf16[1,450,128]{2,1,0:T(8,128)(2,1)S(1)}, u32[]{:S(2)}, u32[]{:S(2)}) collective-permute-start(bf16[1,450,128]{2,1,0:T(8,128)(2,1)} %own_ref.1), channel_id=1, source_target_pairs={{0,2},{1,3},{2,0},{3,1},{4,6},{5,7},{6,4},{7,5},{8,10},{9,11},{10,... | collective-permute-start | bytes 345608 | tf_op jit(solution)/shard_map/ppermute | solution.py:232
  3.0 2.6 %collective-permute-start.1 = (bf16[1,450,128]{2,1,0:T(8,128)(2,1)}, bf16[1,450,128]{2,1,0:T(8,128)(2,1)S(1)}, u32[]{:S(2)}, u32[]{:S(2)}) collective-permute-start(bf16[1,450,128]{2,1,0:T(8,128)(2,1)} %own_ref.1), channel_id=1, source_target_pairs={{0,4},{1,5},{2,6},{3,7},{4,0},{5,1},{6,2},{7,3},{8,12},{9,13},{10,... | collective-permute-start | bytes 345608 | tf_op jit(solution)/shard_map/ppermute | solution.py:232
  5.6 0.0 collective-permute-start.2
  5.6 2.3 %select_weights.1 = (bf16[8,264,128]{2,1,0:T(8,128)(2,1)}, bf16[264,128]{1,0:T(8,128)(2,1)}, bf16[264,128]{1,0:T(8,128)(2,1)}) custom-call(s32[2,4]{1,0:T(2,128)} %bitcast.5, s32[4,128]{1,0:T(4,128)} %bitcast.4, bf16[4,2,128,128]{3,2,1,0:T(8,128)(2,1)} %weight_hbm.1), custom_call_target="tpu_custom_call" | custom-call | flops 276824064 | bytes 540672 | tf_op jit(solution)/shard_map/select_weights/pallas_call | solution.py:262
  8.0 0.0 copy-start.2
  8.0 0.0 collective-permute-done.in_ref
  8.0 5.2 %all-to-all-start = ((bf16[8,264,128]{2,1,0:T(8,128)(2,1)}), bf16[8,264,128]{2,1,0:T(8,128)(2,1)S(1)}, u32[]{:S(2)}, u32[]{:S(2)}) async-start(bf16[8,264,128]{2,1,0:T(8,128)(2,1)} %get-tuple-element.17), calls=%async_computation | async-start | bytes 1081344 | tf_op jit(solution)/shard_map/all_to_all | solution.py:303
  13.2 0.0 copy-start.3
  13.2 0.0 copy-start
  13.2 0.0 copy-start.1
  13.2 1.9 %collective-permute-done.1.far_ref = bf16[1,450,128]{2,1,0:T(8,128)(2,1)S(1)} collective-permute-done((bf16[1,450,128]{2,1,0:T(8,128)(2,1)}, bf16[1,450,128]{2,1,0:T(8,128)(2,1)S(1)}, u32[]{:S(2)}, u32[]{:S(2)}) %collective-permute-start.1) | collective-permute-done | bytes 115232 | tf_op jit(solution)/shard_map/ppermute | solution.py:232
  15.1 0.0 collective-permute-done.2.last_ref
  15.1 0.0 copy-done.2
  15.2 0.1 collective-permute-start.5
  15.2 2.5 %collective-permute-start.4 = (bf16[1,450,128]{2,1,0:T(8,128)(2,1)S(1)}, bf16[1,450,128]{2,1,0:T(8,128)(2,1)S(1)}, u32[]{:S(2)}, u32[]{:S(2)}) collective-permute-start(bf16[1,450,128]{2,1,0:T(8,128)(2,1)S(1)} %get-tuple-element.24), channel_id=1, source_target_pairs={{0,24},{1,9},{2,26},{3,11},{4,28},{5,13},{6,30},{7,15},{8,0},{9,17... | collective-permute-start | bytes 345608 | tf_op jit(solution)/shard_map/ppermute | solution.py:242
  17.7 3.3 %collective-permute-done.4.rim_ref = bf16[1,450,128]{2,1,0:T(8,128)(2,1)S(1)} collective-permute-done((bf16[1,450,128]{2,1,0:T(8,128)(2,1)S(1)}, bf16[1,450,128]{2,1,0:T(8,128)(2,1)S(1)}, u32[]{:S(2)}, u32[]{:S(2)}) %collective-permute-start.4) | collective-permute-done | bytes 115232 | tf_op jit(solution)/shard_map/ppermute | solution.py:242
  21.0 0.0 collective-permute-start.6
  21.0 0.0 copy-done.3
  21.0 0.5 %collective-permute-start.3 = (bf16[264,128]{1,0:T(8,128)(2,1)S(1)}, bf16[264,128]{1,0:T(8,128)(2,1)S(1)}, u32[]{:S(2)}, u32[]{:S(2)}) collective-permute-start(bf16[264,128]{1,0:T(8,128)(2,1)S(1)} %copy-done.3), channel_id=1, source_target_pairs={{0,1},{1,0},{2,3},{3,2},{4,5},{5,4},{6,7},{7,6},{8,9},{9,8},{10,11... | collective-permute-start | bytes 202760 | tf_op jit(solution)/shard_map/ppermute | solution.py:232
  21.5 0.0 copy-done
  21.5 0.2 lay_remap.1.remap_ref
  21.8 0.7 %collective-permute-done.3.crossed_ref = bf16[264,128]{1,0:T(8,128)(2,1)S(1)} collective-permute-done((bf16[264,128]{1,0:T(8,128)(2,1)S(1)}, bf16[264,128]{1,0:T(8,128)(2,1)S(1)}, u32[]{:S(2)}, u32[]{:S(2)}) %collective-permute-start.3) | collective-permute-done | bytes 67616 | tf_op jit(solution)/shard_map/ppermute | solution.py:232
  22.4 0.0 collective-permute-done.6.other_rim_ref
  22.4 0.0 collective-permute-done.5.other_ref
  22.4 0.0 copy-done.1
  22.4 1.8 %begin.1 = (bf16[464,1280]{1,0:T(8,128)(2,1)S(1)}, bf16[5,400,1024]{2,1,0:T(8,128)(2,1)}) custom-call(bf16[264,128]{1,0:T(8,128)(2,1)S(1)} %copy-done.1, bf16[264,128]{1,0:T(8,128)(2,1)S(1)} %collective-permute-done.3.crossed_ref, bf16[4,450,128]{2,1,0:T(8,128)(2,1)S(1)} %get-tuple-element.23.held_ref, ...), custom_call_target="tpu_custom_call" | custom-call | flops 210124800 | bytes 4096000 | tf_op jit(solution)/shard_map/begin/pallas_call | solution.py:322
  24.3 4.6 %all-to-all-done.inbox_ref = bf16[8,264,128]{2,1,0:T(8,128)(2,1)S(1)} async-done(((bf16[8,264,128]{2,1,0:T(8,128)(2,1)}), bf16[8,264,128]{2,1,0:T(8,128)(2,1)S(1)}, u32[]{:S(2)}, u32[]{:S(2)}) %all-to-all-start) | async-done | bytes 540704 | tf_op jit(solution)/shard_map/all_to_all | solution.py:303
  28.9 2.6 %finish.1 = bf16[5,400,1024]{2,1,0:T(8,128)(2,1)} custom-call(bf16[8,264,128]{2,1,0:T(8,128)(2,1)S(1)} %all-to-all-done.inbox_ref, bf16[464,1280]{1,0:T(8,128)(2,1)S(1)} %get-tuple-element.25.parents_ref, bf16[5,400,112]{2,1,0:T(8,128)(2,1)S(1)} %lay_remap.1.remap_ref, bf16[5,400,1024]{2,1,0:T(8,128)(2,1)} %get-tuple-element.26.begun_hbm), custom_call_target="tpu_custom_call", output_to_operand_aliasing={{}: (3, {})} | custom-call | flops 630374400 | bytes 4096000 | tf_op jit(solution)/shard_map/finish/pallas_call | solution.py:343
  (2 shorter events, 0.0 us)
Async XLA Ops:
  0.0 8.0 %collective-permute-start = (bf16[1,450,128]{2,1,0:T(8,128)(2,1)}, bf16[1,450,128]{2,1,0:T(8,128)(2,1)S(1)}, u32[]{:S(2)}, u32[]{:S(2)}) collective-permute-start(bf16[1,450,128]{2,1,0:T(8,128)(2,1)} %own_ref.1), channel_id=1, source_target_pairs={{0,2},{1,3},{2,0},{3,1},{4,6},{5,7},{6,4},{7,5},{8,10},{9,11},{10,... | collective-permute-start | bytes 345608 | tf_op jit(solution)/shard_map/ppermute | solution.py:232
  3.0 12.1 %collective-permute-start.1 = (bf16[1,450,128]{2,1,0:T(8,128)(2,1)}, bf16[1,450,128]{2,1,0:T(8,128)(2,1)S(1)}, u32[]{:S(2)}, u32[]{:S(2)}) collective-permute-start(bf16[1,450,128]{2,1,0:T(8,128)(2,1)} %own_ref.1), channel_id=1, source_target_pairs={{0,4},{1,5},{2,6},{3,7},{4,0},{5,1},{6,2},{7,3},{8,12},{9,13},{10,... | collective-permute-start | bytes 345608 | tf_op jit(solution)/shard_map/ppermute | solution.py:232
  5.6 9.5 %collective-permute-start.2 = (bf16[1,450,128]{2,1,0:T(8,128)(2,1)}, bf16[1,450,128]{2,1,0:T(8,128)(2,1)S(1)}, u32[]{:S(2)}, u32[]{:S(2)}) collective-permute-start(bf16[1,450,128]{2,1,0:T(8,128)(2,1)} %own_ref.1), channel_id=1, source_target_pairs={{0,6},{1,7},{2,4},{3,5},{4,2},{5,3},{6,0},{7,1},{8,14},{9,15},{10,... | collective-permute-start | bytes 345608 | tf_op jit(solution)/shard_map/ppermute | solution.py:232
  8.0 7.2 %copy-start.2 = (bf16[1,450,128]{2,1,0:T(8,128)(2,1)S(1)}, bf16[1,450,128]{2,1,0:T(8,128)(2,1)}, u32[]{:S(2)}) copy-start(bf16[1,450,128]{2,1,0:T(8,128)(2,1)} %own_ref.1) | copy-start | bytes 345604
  8.0 20.9 %all-to-all-start = ((bf16[8,264,128]{2,1,0:T(8,128)(2,1)}), bf16[8,264,128]{2,1,0:T(8,128)(2,1)S(1)}, u32[]{:S(2)}, u32[]{:S(2)}) async-start(bf16[8,264,128]{2,1,0:T(8,128)(2,1)} %get-tuple-element.17), calls=%async_computation | async-start | bytes 1081344 | tf_op jit(solution)/shard_map/all_to_all | solution.py:303
  13.2 7.8 %copy-start.3 = (bf16[264,128]{1,0:T(8,128)(2,1)S(1)}, bf16[264,128]{1,0:T(8,128)(2,1)}, u32[]{:S(2)}) copy-start(bf16[264,128]{1,0:T(8,128)(2,1)} %get-tuple-element.22) | copy-start | bytes 202756
  13.2 8.3 %copy-start = (bf16[5,400,90]{1,2,0:T(8,128)(2,1)S(1)}, bf16[5,400,90]{1,2,0:T(8,128)(2,1)}, u32[]{:S(2)}) copy-start(bf16[5,400,90]{1,2,0:T(8,128)(2,1)} %param.9) | copy-start | bytes 1080004
  13.2 9.2 %copy-start.1 = (bf16[264,128]{1,0:T(8,128)(2,1)S(1)}, bf16[264,128]{1,0:T(8,128)(2,1)}, u32[]{:S(2)}) copy-start(bf16[264,128]{1,0:T(8,128)(2,1)} %get-tuple-element.18.own_ref) | copy-start | bytes 202756
  15.2 7.3 %collective-permute-start.5 = (bf16[4,450,128]{2,1,0:T(8,128)(2,1)S(1)}, bf16[4,450,128]{2,1,0:T(8,128)(2,1)S(1)}, u32[]{:S(2)}, u32[]{:S(2)}) collective-permute-start(bf16[4,450,128]{2,1,0:T(8,128)(2,1)S(1)} %get-tuple-element.23.held_ref), channel_id=1, source_target_pairs={{0,1},{1,0},{2,3},{3,2},{4,5},{5,4},{6,7},{7,6},{8,9},{9,8},{10,11... | collective-permute-start | bytes 1382408 | tf_op jit(solution)/shard_map/ppermute | solution.py:232
  15.2 5.8 %collective-permute-start.4 = (bf16[1,450,128]{2,1,0:T(8,128)(2,1)S(1)}, bf16[1,450,128]{2,1,0:T(8,128)(2,1)S(1)}, u32[]{:S(2)}, u32[]{:S(2)}) collective-permute-start(bf16[1,450,128]{2,1,0:T(8,128)(2,1)S(1)} %get-tuple-element.24), channel_id=1, source_target_pairs={{0,24},{1,9},{2,26},{3,11},{4,28},{5,13},{6,30},{7,15},{8,0},{9,17... | collective-permute-start | bytes 345608 | tf_op jit(solution)/shard_map/ppermute | solution.py:242
  21.0 1.4 %collective-permute-start.6 = (bf16[1,450,128]{2,1,0:T(8,128)(2,1)S(1)}, bf16[1,450,128]{2,1,0:T(8,128)(2,1)S(1)}, u32[]{:S(2)}, u32[]{:S(2)}) collective-permute-start(bf16[1,450,128]{2,1,0:T(8,128)(2,1)S(1)} %collective-permute-done.4.rim_ref), channel_id=1, source_target_pairs={{0,1},{1,0},{2,3},{3,2},{4,5},{5,4},{6,7},{7,6},{8,9},{9,8},{10,11... | collective-permute-start | bytes 345608 | tf_op jit(solution)/shard_map/ppermute | solution.py:232
  21.0 1.4 %collective-permute-start.3 = (bf16[264,128]{1,0:T(8,128)(2,1)S(1)}, bf16[264,128]{1,0:T(8,128)(2,1)S(1)}, u32[]{:S(2)}, u32[]{:S(2)}) collective-permute-start(bf16[264,128]{1,0:T(8,128)(2,1)S(1)} %copy-done.3), channel_id=1, source_target_pairs={{0,1},{1,0},{2,3},{3,2},{4,5},{5,4},{6,7},{7,6},{8,9},{9,8},{10,11... | collective-permute-start | bytes 202760 | tf_op jit(solution)/shard_map/ppermute | solution.py:232
